TPU v7x, 256 devices: a whole 4x4x8 slice. The times are simulated.
256 devices in a mesh: rows: 16 (over y, z_lo), cols: 16 (over x, z_hi, core).
Axes of the slice: x: 4, y: 4, z: 8 (z_hi: 2, z_lo: 4; z = z_hi * 4 + z_lo), core: 2. Of those that a mesh axis runs over, the one named last changes fastest.
Arguments:
- activations: bfloat16 [256, 256, 384], P('rows', 'cols'), may hold values from -6 to 6
- grad_out: bfloat16 [256, 256, 384], P('rows', 'cols'), may hold values from -6 to 6
- kernels: float32 [2, 7, 7, 384], replicated, may hold values from -0.875 to 0.875
- norm_gains: float32 [2, 384], replicated, may hold values from 0.5 to 1.5
- norm_shifts: float32 [2, 384], replicated, may hold values from -3 to 3
- w_in: bfloat16 [2, 384, 1536], replicated, may hold values from -0.3125 to 0.3125
- b_in: float32 [2, 1536], replicated, may hold values from -3 to 3
- w_out: bfloat16 [2, 384, 1536], replicated, may hold values from -0.15625 to 0.15625
Outputs:
- grad_in: bfloat16 [256, 256, 384], P('rows', 'cols')
- grad_kernels: float32 [2, 7, 7, 384], replicated
- grad_gains: float32 [2, 384], replicated
- grad_shifts: float32 [2, 384], replicated
- grad_b_in: float32 [2, 1536], replicated
- grad_w_in: float32 [2, 384, 1536], P(None, None, ('rows', 'cols'))
- grad_w_out: float32 [2, 384, 1536], P(None, None, ('rows', 'cols'))
All inputs are finite; a program needn't handle non-finite values.
Results may differ from a plain program's by a relative error of at most 0.017.
Values may be sent and summed in bfloat16 or wider, within the bound.
A program may use at most 128 MiB of HBM per device.

v0:
```python
import math

import jax
import jax.numpy as jnp
from jax import lax
from jax.sharding import PartitionSpec as P

EPSILON = 1e-06
ROOT_HALF = 0.7071067811865476
INV_ROOT_TAU = 0.3989422804014327


def with_halo(block, sides, width):
    for axis, dim in sides:
        count = lax.axis_size(axis)
        forward = [(i, i + 1) for i in range(count - 1)]
        backward = [(target, source) for source, target in forward]
        low = lax.ppermute(
            lax.slice_in_dim(block, block.shape[dim] - width, None, axis=dim), axis, forward
        )
        high = lax.ppermute(lax.slice_in_dim(block, 0, width, axis=dim), axis, backward)
        block = jnp.concatenate([low, block, high], axis=dim)
    return block


def gelu_parts(pre_act):
    normal_cdf = 0.5 * (1.0 + lax.erf(pre_act * ROOT_HALF))
    density = jnp.exp(-0.5 * pre_act * pre_act) * INV_ROOT_TAU
    return (pre_act * normal_cdf, normal_cdf + pre_act * density)


def conv_from(padded, kernel, out_rows, out_cols):
    running = jnp.zeros((out_rows, out_cols, padded.shape[2]), jnp.float32)
    for row_off in range(7):
        for col_off in range(7):
            running = (
                running
                + kernel[row_off, col_off]
                * padded[row_off : row_off + out_rows, col_off : col_off + out_cols]
            )
    return running


def conv_back(padded_grad, kernel, out_rows, out_cols):
    running = jnp.zeros((out_rows, out_cols, padded_grad.shape[2]), jnp.float32)
    for row_off in range(7):
        for col_off in range(7):
            running = (
                running
                + kernel[row_off, col_off]
                * padded_grad[
                    6 - row_off : 6 - row_off + out_rows, 6 - col_off : 6 - col_off + out_cols
                ]
            )
    return running


def kernel_grad(grad_z, padded_in):
    out_rows, out_cols = (grad_z.shape[0], grad_z.shape[1])
    kernel_taps = []
    for row_off in range(7):
        for col_off in range(7):
            kernel_taps.append(
                jnp.sum(
                    grad_z * padded_in[row_off : row_off + out_rows, col_off : col_off + out_cols],
                    axis=(0, 1),
                )
            )
    return jnp.stack(kernel_taps).reshape(7, 7, grad_z.shape[2])


def norm_fwd(source, gain, shift):
    center = source - jnp.mean(source, axis=-1, keepdims=True)
    inv_std = lax.rsqrt(jnp.mean(center * center, axis=-1, keepdims=True) + EPSILON)
    norm_hat = center * inv_std
    return (norm_hat, inv_std, (norm_hat * gain + shift).astype(jnp.bfloat16))


def norm_back(grad_n, norm_hat, inv_std, gain):
    scaled = grad_n * gain
    return inv_std * (
        scaled
        - jnp.mean(scaled, axis=-1, keepdims=True)
        - norm_hat * jnp.mean(scaled * norm_hat, axis=-1, keepdims=True)
    )


def mlp_hidden(normed_flat, weight_in, bias_in):
    pre_act = jnp.dot(normed_flat, weight_in, preferred_element_type=jnp.float32) + bias_in
    activation, gelu_slope = gelu_parts(pre_act)
    return (activation.astype(jnp.bfloat16), gelu_slope)


def mlp_forward(normed_flat, weight_in, bias_in, weight_out):
    act_b, gelu_slope = mlp_hidden(normed_flat, weight_in, bias_in)
    mixed = lax.dot_general(
        act_b, weight_out, (((1,), (1,)), ((), ())), preferred_element_type=jnp.float32
    )
    return (act_b, gelu_slope, mixed)


def input_rim(source):
    return with_halo(source, (("rows", 0), ("cols", 1)), 3)


def layer_back(
    grad_b,
    normed_flat,
    act_b,
    gelu_slope,
    norm_hat,
    inv_std,
    kernel,
    gain,
    weight_in,
    weight_out,
    padded_in,
):
    tile_rows, tile_cols, channels = grad_b.shape
    grad_flat = grad_b.reshape(-1, channels)
    grad_wo = lax.dot_general(
        grad_flat, act_b, (((0,), (0,)), ((), ())), preferred_element_type=jnp.float32
    )
    grad_pre = jnp.dot(grad_flat, weight_out, preferred_element_type=jnp.float32) * gelu_slope
    grad_preb = grad_pre.astype(jnp.bfloat16)
    grad_wi = lax.dot_general(
        normed_flat, grad_preb, (((0,), (0,)), ((), ())), preferred_element_type=jnp.float32
    )
    grad_bias = jnp.sum(grad_pre, axis=0)
    grad_n = lax.dot_general(
        grad_preb, weight_in, (((1,), (1,)), ((), ())), preferred_element_type=jnp.float32
    ).reshape(grad_b.shape)
    grad_gain = jnp.sum(grad_n * norm_hat, axis=(0, 1))
    grad_shift = jnp.sum(grad_n, axis=(0, 1))
    grad_z = norm_back(grad_n, norm_hat, inv_std, gain).astype(jnp.bfloat16)
    padded_grad = with_halo(grad_z, (("rows", 0), ("cols", 1)), 3)
    kernel_taps = kernel_grad(grad_z.astype(jnp.float32), padded_in)
    spread = conv_back(padded_grad.astype(jnp.float32), kernel, tile_rows, tile_cols)
    return (spread, kernel_taps, grad_gain, grad_shift, grad_bias, grad_wi, grad_wo)


def shards(activations, grad_out, kernels, norm_gains, norm_shifts, w_in, b_in, w_out):
    tile_rows, tile_cols, channels = activations.shape
    grad_scale = 1.0 / math.sqrt(
        tile_rows * tile_cols * lax.axis_size("rows") * lax.axis_size("cols")
    )
    padded_in = input_rim(activations).astype(jnp.float32)
    conv_one = conv_from(padded_in, kernels[0], tile_rows, tile_cols)
    hat_one, inv_one, normed_grid = norm_fwd(conv_one, norm_gains[0], norm_shifts[0])
    normed_one = normed_grid.reshape(-1, channels)
    act_one, slope_one, mixed_one = mlp_forward(normed_one, w_in[0], b_in[0], w_out[0])
    middle = (activations.astype(jnp.float32) + mixed_one.reshape(activations.shape)).astype(
        jnp.bfloat16
    )
    padded_mid = input_rim(middle)
    padded_mid_wide = padded_mid.astype(jnp.float32)
    conv_two = conv_from(padded_mid_wide, kernels[1], tile_rows, tile_cols)
    hat_two, inv_two, normed_grid_two = norm_fwd(conv_two, norm_gains[1], norm_shifts[1])
    normed_two = normed_grid_two.reshape(-1, channels)
    act_two, slope_two = mlp_hidden(normed_two, w_in[1], b_in[1])
    back_two = layer_back(
        grad_out,
        normed_two,
        act_two,
        slope_two,
        hat_two,
        inv_two,
        kernels[1],
        norm_gains[1],
        w_in[1],
        w_out[1],
        padded_mid_wide,
    )
    grad_mid = (grad_out.astype(jnp.float32) + back_two[0]).astype(jnp.bfloat16)
    back_one = layer_back(
        grad_mid,
        normed_one,
        act_one,
        slope_one,
        hat_one,
        inv_one,
        kernels[0],
        norm_gains[0],
        w_in[0],
        w_out[0],
        padded_in,
    )
    grad_in = (grad_mid.astype(jnp.float32) + back_one[0]).astype(jnp.bfloat16)
    grad_kernels, grad_gains, grad_shifts, grad_b_in = lax.psum(
        (
            jnp.stack([back_one[1], back_two[1]]) * grad_scale,
            jnp.stack([back_one[2], back_two[2]]) * grad_scale,
            jnp.stack([back_one[3], back_two[3]]) * grad_scale,
            jnp.stack([back_one[4], back_two[4]]) * grad_scale,
        ),
        ("rows", "cols"),
    )
    stacked_in = jnp.stack([back_one[5], back_two[5]]) * grad_scale
    stacked_out = jnp.stack([back_one[6], back_two[6]]) * grad_scale
    grad_w_in, grad_w_out = (
        lax.psum_scatter(stacked_in, ("rows", "cols"), scatter_dimension=2, tiled=True),
        lax.psum_scatter(stacked_out, ("rows", "cols"), scatter_dimension=2, tiled=True),
    )
    return (grad_in, grad_kernels, grad_gains, grad_shifts, grad_b_in, grad_w_in, grad_w_out)


def solution(mesh):
    return jax.shard_map(
        shards,
        mesh=mesh,
        in_specs=(P("rows", "cols", None), P("rows", "cols", None), P(), P(), P(), P(), P(), P()),
        out_specs=(
            P("rows", "cols", None),
            P(),
            P(),
            P(),
            P(),
            P(None, None, ("rows", "cols")),
            P(None, None, ("rows", "cols")),
        ),
        check_vma=False,
    )
```

profile of v0, /device:TPU:1, one launch (start us, length us, event | category | flops | bytes accessed | tf_op | source)
XLA Modules:
  0.0 460.2 jit_solution(10851110256736545179)
XLA Ops:
  9.3 5.0 %collective-permute-start = (bf16[3,16,384]{2,1,0:T(8,128)(2,1)S(1)}, bf16[3,16,384]{2,1,0:T(8,128)(2,1)S(1)}, u32[]{:S(2)}, u32[]{:S(2)}) collective-permute-start(bf16[3,16,384]{2,1,0:T(8,128)(2,1)S(1)} %get-tuple-element.269), channel_id=1, source_target_pairs={{0,16},{16,32},{32,48},{48,64},{64,80},{80,96},{96,112},{112,128},... | collective-permute-start | bytes 110600 | tf_op jit(solution)/shard_map/ppermute | solution.py:18
  19.3 9.8 %collective-permute-start.2 = (bf16[22,3,384]{2,1,0:T(4,128)(2,1)S(1)}, bf16[22,3,384]{2,1,0:T(4,128)(2,1)S(1)}, u32[]{:S(2)}, u32[]{:S(2)}) collective-permute-start(bf16[22,3,384]{2,1,0:T(4,128)(2,1)S(1)} %get-tuple-element.260), channel_id=1, source_target_pairs={{0,1},{1,2},{2,3},{3,4},{4,5},{5,6},{6,7},{7,8},{8,9},{9,10},{10,1... | collective-permute-start | bytes 152072 | tf_op jit(solution)/shard_map/ppermute | solution.py:18
  29.0 1.9 collective-permute-start.3
  31.6 7.0 %collective-permute-done.3 = bf16[22,3,384]{2,1,0:T(4,128)(2,1)S(1)} collective-permute-done((bf16[22,3,384]{2,1,0:T(4,128)(2,1)S(1)}, bf16[22,3,384]{2,1,0:T(4,128)(2,1)S(1)}, u32[]{:S(2)}, u32[]{:S(2)}) %collective-permute-start.3) | collective-permute-done | bytes 50720 | tf_op jit(solution)/shard_map/ppermute | solution.py:21
  38.7 3.8 fusion.226
  46.9 2.6 collective-permute-start.4
  51.2 3.1 collective-permute-done.5
  54.3 3.3 collective-permute-start.6
  57.6 1.9 collective-permute-start.7
  59.8 7.9 %collective-permute-done.7 = bf16[22,3,384]{2,1,0:T(4,128)(2,1)S(1)} collective-permute-done((bf16[22,3,384]{2,1,0:T(4,128)(2,1)S(1)}, bf16[22,3,384]{2,1,0:T(4,128)(2,1)S(1)}, u32[]{:S(2)}, u32[]{:S(2)}) %collective-permute-start.7) | collective-permute-done | bytes 50720 | tf_op jit(solution)/shard_map/ppermute | solution.py:21
  67.8 3.6 fusion.225
  78.0 4.3 collective-permute-start.8
  83.7 2.0 convolution_bitcast_fusion
  85.8 1.8 collective-permute-done.9
  88.3 3.0 collective-permute-start.10
  91.3 1.9 collective-permute-start.11
  110.0 4.3 stack.447
  115.5 3.9 fusion.177
  121.2 1.9 multiply_reduce_fusion.1
  126.4 1.9 convolution_bitcast_fusion.1
  128.3 1.9 convolution_bitcast_fusion.3
  131.0 5.0 %maximum_multiply_fusion.1 = f32[2,384,1536]{2,1,0:T(8,128)} fusion(f32[1,384,1536]{2,1,0:T(8,128)} %convolution_bitcast_fusion, f32[1,384,1536]{2,1,0:T(8,128)} %convolution_bitcast_fusion.1), kind=kLoop, calls=%fused_computation.99 | loop fusion | flops 2359296 | bytes 9437184 | tf_op jit(solution)/shard_map/mul | solution.py:199
  136.0 8.2 %copy.28 = f32[2,384,1536]{1,0,2:T(2,128)} copy(f32[2,384,1536]{2,1,0:T(8,128)} %maximum_multiply_fusion.1) | data formatting | bytes 9437184 | tf_op jit(solution)/shard_map/mul | solution.py:199
  144.1 4.5 maximum_multiply_fusion
  148.6 8.2 %copy.26 = f32[2,384,1536]{1,0,2:T(2,128)} copy(f32[2,384,1536]{2,1,0:T(8,128)} %maximum_multiply_fusion) | data formatting | bytes 9437184 | tf_op jit(solution)/shard_map/mul | solution.py:198
  160.2 6.3 %collective-permute-start.12 = (bf16[3,16,384]{2,1,0:T(8,128)(2,1)S(1)}, bf16[3,16,384]{2,1,0:T(8,128)(2,1)S(1)}, u32[]{:S(2)}, u32[]{:S(2)}) collective-permute-start(bf16[3,16,384]{2,1,0:T(8,128)(2,1)S(1)} %get-tuple-element.262), channel_id=1, source_target_pairs={{0,16},{16,32},{32,48},{48,64},{64,80},{80,96},{96,112},{112,128},... | collective-permute-start | bytes 110600 | tf_op jit(solution)/shard_map/ppermute | solution.py:18
  168.6 3.3 collective-permute-done.13
  172.0 8.7 %collective-permute-start.14 = (bf16[22,3,384]{2,1,0:T(4,128)(2,1)S(1)}, bf16[22,3,384]{2,1,0:T(4,128)(2,1)S(1)}, u32[]{:S(2)}, u32[]{:S(2)}) collective-permute-start(bf16[22,3,384]{2,1,0:T(4,128)(2,1)S(1)} %get-tuple-element.254), channel_id=1, source_target_pairs={{0,1},{1,2},{2,3},{3,4},{4,5},{5,6},{6,7},{7,8},{8,9},{9,10},{10,1... | collective-permute-start | bytes 152072 | tf_op jit(solution)/shard_map/ppermute | solution.py:18
  180.7 1.9 collective-permute-start.15
  182.7 84.4 %all-reduce.2 = (f32[2,384]{1,0:T(2,128)}, f32[2,384]{1,0:T(2,128)}, f32[2,1536]{1,0:T(2,128)}) all-reduce(f32[2,384]{1,0:T(2,128)S(1)} %maximum_multiply_fusion.4, f32[2,384]{1,0:T(2,128)S(1)} %maximum_multiply_fusion.5, f32[2,1536]{1,0:T(2,128)S(1)} %maximum_multiply_fusion.3), channel_id=1, replica_groups=mesh['rows'=16,'cols'=16] {'rows','cols'}, use_global_device_ids=true, to_apply=%region_109.0 | all-reduce | flops 4608 | bytes 36864 | tf_op jit(solution)/shard_map/psum | solution.py:189
  267.6 4.2 fusion.127
  271.8 177.2 %all-reduce.6.cloned.1.call-done = (f32[2,7,7,384]{3,2,1,0:T(8,128)}, f32[2,384,1536]{1,0,2:T(2,128)}, f32[2,384,1536]{1,0,2:T(2,128)}) async-done(((f32[2,7,7,384]{3,2,1,0:T(8,128)}, f32[2,384,1536]{1,0,2:T(2,128)}, f32[2,384,1536]{1,0,2:T(2,128)}), (f32[2,7,7,384]{3,2,1,0:T(8,128)}, f32[2,384,1536]{1,0,2:T(2,128)}, f32[2,384,1536]{1,0,2:T(2,128)})) %all-reduce.6.cloned.1.call-update) | async-done | bytes 9587728 | tf_op jit(solution)/shard_map/psum | solution.py:189
  (433 shorter events, 54.8 us)
Async XLA Ops:
  7.2 441.8 %all-reduce.6.cloned.1.call-start = ((), (), s32[]{:S(2)}) async-start(), calls=%async_computation | async-start | bytes 19218432 | tf_op jit(solution)/shard_map/psum | solution.py:189
  8.0 11.2 %collective-permute-start.1 = (bf16[3,16,384]{2,1,0:T(8,128)(2,1)S(1)}, bf16[3,16,384]{2,1,0:T(8,128)(2,1)S(1)}, u32[]{:S(2)}, u32[]{:S(2)}) collective-permute-start(bf16[3,16,384]{2,1,0:T(8,128)(2,1)S(1)} %get-tuple-element.268), channel_id=1, source_target_pairs={{16,0},{32,16},{48,32},{64,48},{80,64},{96,80},{112,96},{128,112},... | collective-permute-start | bytes 110600 | tf_op jit(solution)/shard_map/ppermute | solution.py:21
  9.3 8.9 %collective-permute-start = (bf16[3,16,384]{2,1,0:T(8,128)(2,1)S(1)}, bf16[3,16,384]{2,1,0:T(8,128)(2,1)S(1)}, u32[]{:S(2)}, u32[]{:S(2)}) collective-permute-start(bf16[3,16,384]{2,1,0:T(8,128)(2,1)S(1)} %get-tuple-element.269), channel_id=1, source_target_pairs={{0,16},{16,32},{32,48},{48,64},{64,80},{80,96},{96,112},{112,128},... | collective-permute-start | bytes 110600 | tf_op jit(solution)/shard_map/ppermute | solution.py:18
  19.3 12.3 %collective-permute-start.2 = (bf16[22,3,384]{2,1,0:T(4,128)(2,1)S(1)}, bf16[22,3,384]{2,1,0:T(4,128)(2,1)S(1)}, u32[]{:S(2)}, u32[]{:S(2)}) collective-permute-start(bf16[22,3,384]{2,1,0:T(4,128)(2,1)S(1)} %get-tuple-element.260), channel_id=1, source_target_pairs={{0,1},{1,2},{2,3},{3,4},{4,5},{5,6},{6,7},{7,8},{8,9},{9,10},{10,1... | collective-permute-start | bytes 152072 | tf_op jit(solution)/shard_map/ppermute | solution.py:18
  29.0 9.5 %collective-permute-start.3 = (bf16[22,3,384]{2,1,0:T(4,128)(2,1)S(1)}, bf16[22,3,384]{2,1,0:T(4,128)(2,1)S(1)}, u32[]{:S(2)}, u32[]{:S(2)}) collective-permute-start(bf16[22,3,384]{2,1,0:T(4,128)(2,1)S(1)} %get-tuple-element.261), channel_id=1, source_target_pairs={{1,0},{2,1},{3,2},{4,3},{5,4},{6,5},{7,6},{8,7},{9,8},{10,9},{11,1... | collective-permute-start | bytes 152072 | tf_op jit(solution)/shard_map/ppermute | solution.py:21
  46.9 4.3 collective-permute-start.4
  49.6 4.7 %collective-permute-start.5 = (bf16[3,16,384]{2,1,0:T(8,128)(2,1)S(1)}, bf16[3,16,384]{2,1,0:T(8,128)(2,1)S(1)}, u32[]{:S(2)}, u32[]{:S(2)}) collective-permute-start(bf16[3,16,384]{2,1,0:T(8,128)(2,1)S(1)} %get-tuple-element.267), channel_id=1, source_target_pairs={{16,0},{32,16},{48,32},{64,48},{80,64},{96,80},{112,96},{128,112},... | collective-permute-start | bytes 110600 | tf_op jit(solution)/shard_map/ppermute | solution.py:21
  54.3 5.4 %collective-permute-start.6 = (bf16[22,3,384]{2,1,0:T(4,128)(2,1)S(1)}, bf16[22,3,384]{2,1,0:T(4,128)(2,1)S(1)}, u32[]{:S(2)}, u32[]{:S(2)}) collective-permute-start(bf16[22,3,384]{2,1,0:T(4,128)(2,1)S(1)} %get-tuple-element.258), channel_id=1, source_target_pairs={{0,1},{1,2},{2,3},{3,4},{4,5},{5,6},{6,7},{7,8},{8,9},{9,10},{10,1... | collective-permute-start | bytes 152072 | tf_op jit(solution)/shard_map/ppermute | solution.py:18
  57.6 10.0 %collective-permute-start.7 = (bf16[22,3,384]{2,1,0:T(4,128)(2,1)S(1)}, bf16[22,3,384]{2,1,0:T(4,128)(2,1)S(1)}, u32[]{:S(2)}, u32[]{:S(2)}) collective-permute-start(bf16[22,3,384]{2,1,0:T(4,128)(2,1)S(1)} %get-tuple-element.259), channel_id=1, source_target_pairs={{1,0},{2,1},{3,2},{4,3},{5,4},{6,5},{7,6},{8,7},{9,8},{10,9},{11,1... | collective-permute-start | bytes 152072 | tf_op jit(solution)/shard_map/ppermute | solution.py:21
  78.0 7.8 %collective-permute-start.8 = (bf16[3,16,384]{2,1,0:T(8,128)(2,1)S(1)}, bf16[3,16,384]{2,1,0:T(8,128)(2,1)S(1)}, u32[]{:S(2)}, u32[]{:S(2)}) collective-permute-start(bf16[3,16,384]{2,1,0:T(8,128)(2,1)S(1)} %get-tuple-element.264), channel_id=1, source_target_pairs={{0,16},{16,32},{32,48},{48,64},{64,80},{80,96},{96,112},{112,128},... | collective-permute-start | bytes 110600 | tf_op jit(solution)/shard_map/ppermute | solution.py:18
  82.3 5.3 %collective-permute-start.9 = (bf16[3,16,384]{2,1,0:T(8,128)(2,1)S(1)}, bf16[3,16,384]{2,1,0:T(8,128)(2,1)S(1)}, u32[]{:S(2)}, u32[]{:S(2)}) collective-permute-start(bf16[3,16,384]{2,1,0:T(8,128)(2,1)S(1)} %get-tuple-element.265), channel_id=1, source_target_pairs={{16,0},{32,16},{48,32},{64,48},{80,64},{96,80},{112,96},{128,112},... | collective-permute-start | bytes 110600 | tf_op jit(solution)/shard_map/ppermute | solution.py:21
  88.3 26.0 %collective-permute-start.10 = (bf16[22,3,384]{2,1,0:T(4,128)(2,1)}, bf16[22,3,384]{2,1,0:T(4,128)(2,1)}, u32[]{:S(2)}, u32[]{:S(2)}) collective-permute-start(bf16[22,3,384]{2,1,0:T(4,128)(2,1)} %get-tuple-element.256), channel_id=1, source_target_pairs={{0,1},{1,2},{2,3},{3,4},{4,5},{5,6},{6,7},{7,8},{8,9},{9,10},{10,1... | collective-permute-start | bytes 152072 | tf_op jit(solution)/shard_map/ppermute | solution.py:18
  91.3 23.0 %collective-permute-start.11 = (bf16[22,3,384]{2,1,0:T(4,128)(2,1)}, bf16[22,3,384]{2,1,0:T(4,128)(2,1)}, u32[]{:S(2)}, u32[]{:S(2)}) collective-permute-start(bf16[22,3,384]{2,1,0:T(4,128)(2,1)} %get-tuple-element.257), channel_id=1, source_target_pairs={{1,0},{2,1},{3,2},{4,3},{5,4},{6,5},{7,6},{8,7},{9,8},{10,9},{11,1... | collective-permute-start | bytes 152072 | tf_op jit(solution)/shard_map/ppermute | solution.py:21
  157.5 109.7 %copy-start.3 = (bf16[16,16,384]{2,1,0:T(8,128)(2,1)S(1)}, bf16[16,16,384]{2,1,0:T(8,128)(2,1)}, u32[]{:S(2)}) copy-start(bf16[16,16,384]{2,1,0:T(8,128)(2,1)} %copy-done.2) | copy-start | bytes 589828
  157.5 109.7 %copy-start.15 = (f32[384]{0:T(512)S(1)}, f32[384]{0:T(512)}, u32[]{:S(2)}) copy-start(f32[384]{0:T(512)} %copy-done.14) | copy-start | bytes 4612
  157.5 109.7 %copy-start.17 = (f32[384]{0:T(512)S(1)}, f32[384]{0:T(512)}, u32[]{:S(2)}) copy-start(f32[384]{0:T(512)} %copy-done.16) | copy-start | bytes 4612
  157.5 109.7 %copy-start.19 = (f32[384]{0:T(512)S(1)}, f32[384]{0:T(512)}, u32[]{:S(2)}) copy-start(f32[384]{0:T(512)} %copy-done.18) | copy-start | bytes 4612
  157.6 109.7 %copy-start.21 = (f32[384]{0:T(512)S(1)}, f32[384]{0:T(512)}, u32[]{:S(2)}) copy-start(f32[384]{0:T(512)} %copy-done.20) | copy-start | bytes 4612
  157.6 109.7 %copy-start.23 = (f32[384]{0:T(512)S(1)}, f32[384]{0:T(512)}, u32[]{:S(2)}) copy-start(f32[384]{0:T(512)} %copy-done.22) | copy-start | bytes 4612
  157.6 109.7 %copy-start.25 = (f32[384]{0:T(512)S(1)}, f32[384]{0:T(512)}, u32[]{:S(2)}) copy-start(f32[384]{0:T(512)} %copy-done.24) | copy-start | bytes 4612
  157.6 109.7 %copy-start.27 = (f32[384]{0:T(512)S(1)}, f32[384]{0:T(512)}, u32[]{:S(2)}) copy-start(f32[384]{0:T(512)} %copy-done.26) | copy-start | bytes 4612
  157.6 109.7 %copy-start.29 = (f32[384]{0:T(512)S(1)}, f32[384]{0:T(512)}, u32[]{:S(2)}) copy-start(f32[384]{0:T(512)} %copy-done.28) | copy-start | bytes 4612
  157.6 109.7 %copy-start.31 = (f32[384]{0:T(512)S(1)}, f32[384]{0:T(512)}, u32[]{:S(2)}) copy-start(f32[384]{0:T(512)} %copy-done.30) | copy-start | bytes 4612
  157.6 109.7 %copy-start.33 = (f32[384]{0:T(512)S(1)}, f32[384]{0:T(512)}, u32[]{:S(2)}) copy-start(f32[384]{0:T(512)} %copy-done.32) | copy-start | bytes 4612
  157.6 109.7 %copy-start.35 = (f32[384]{0:T(512)S(1)}, f32[384]{0:T(512)}, u32[]{:S(2)}) copy-start(f32[384]{0:T(512)} %copy-done.34) | copy-start | bytes 4612
  157.6 109.7 %copy-start.37 = (f32[384]{0:T(512)S(1)}, f32[384]{0:T(512)}, u32[]{:S(2)}) copy-start(f32[384]{0:T(512)} %copy-done.36) | copy-start | bytes 4612
  157.6 109.7 %copy-start.39 = (f32[384]{0:T(512)S(1)}, f32[384]{0:T(512)}, u32[]{:S(2)}) copy-start(f32[384]{0:T(512)} %copy-done.38) | copy-start | bytes 4612
  157.7 109.7 %copy-start.41 = (f32[384]{0:T(512)S(1)}, f32[384]{0:T(512)}, u32[]{:S(2)}) copy-start(f32[384]{0:T(512)} %copy-done.40) | copy-start | bytes 4612
  160.2 8.4 %collective-permute-start.12 = (bf16[3,16,384]{2,1,0:T(8,128)(2,1)S(1)}, bf16[3,16,384]{2,1,0:T(8,128)(2,1)S(1)}, u32[]{:S(2)}, u32[]{:S(2)}) collective-permute-start(bf16[3,16,384]{2,1,0:T(8,128)(2,1)S(1)} %get-tuple-element.262), channel_id=1, source_target_pairs={{0,16},{16,32},{32,48},{48,64},{64,80},{80,96},{96,112},{112,128},... | collective-permute-start | bytes 110600 | tf_op jit(solution)/shard_map/ppermute | solution.py:18
  166.6 5.3 %collective-permute-start.13 = (bf16[3,16,384]{2,1,0:T(8,128)(2,1)S(1)}, bf16[3,16,384]{2,1,0:T(8,128)(2,1)S(1)}, u32[]{:S(2)}, u32[]{:S(2)}) collective-permute-start(bf16[3,16,384]{2,1,0:T(8,128)(2,1)S(1)} %get-tuple-element.263), channel_id=1, source_target_pairs={{16,0},{32,16},{48,32},{64,48},{80,64},{96,80},{112,96},{128,112},... | collective-permute-start | bytes 110600 | tf_op jit(solution)/shard_map/ppermute | solution.py:21
  172.0 95.1 %collective-permute-start.14 = (bf16[22,3,384]{2,1,0:T(4,128)(2,1)S(1)}, bf16[22,3,384]{2,1,0:T(4,128)(2,1)S(1)}, u32[]{:S(2)}, u32[]{:S(2)}) collective-permute-start(bf16[22,3,384]{2,1,0:T(4,128)(2,1)S(1)} %get-tuple-element.254), channel_id=1, source_target_pairs={{0,1},{1,2},{2,3},{3,4},{4,5},{5,6},{6,7},{7,8},{8,9},{9,10},{10,1... | collective-permute-start | bytes 152072 | tf_op jit(solution)/shard_map/ppermute | solution.py:18
  180.7 86.4 %collective-permute-start.15 = (bf16[22,3,384]{2,1,0:T(4,128)(2,1)S(1)}, bf16[22,3,384]{2,1,0:T(4,128)(2,1)S(1)}, u32[]{:S(2)}, u32[]{:S(2)}) collective-permute-start(bf16[22,3,384]{2,1,0:T(4,128)(2,1)S(1)} %get-tuple-element.255), channel_id=1, source_target_pairs={{1,0},{2,1},{3,2},{4,3},{5,4},{6,5},{7,6},{8,7},{9,8},{10,9},{11,1... | collective-permute-start | bytes 152072 | tf_op jit(solution)/shard_map/ppermute | solution.py:21
  (111 other events, 4266.3 us)
Sparse Core Ops, SparseCore 0:
  157.6 291.3 all-reduce.5
where the time goes:
time: 463 us; the launch traced here: 460 us
  waiting for transfers between devices  200 us (43%)
  blocking collectives  84.4 us (18%)
  starting transfers between devices  56.1 us (12%)
  local copies, waits for them, and re-layouts  53.2 us (11%)
  other arithmetic  34.6 us (7%)
  between operations  16.8 us (4%)
  matrix products  14.8 us (3%)
    psum x1, waiting for transfers between devices, shards(): lax.psum((jnp.stack([back_one[1], back_two[1]]) * grad_scale, jnp.stack([...  177 us
    psum x1, blocking collectives, shards(): lax.psum((jnp.stack([back_one[1], back_two[1]]) * grad_scale, jnp.stack([...  84.4 us
    ppermute x8, starting transfers between devices, with_halo(): lax.ppermute(lax.slice_in_dim(block, block.shape[dim] - width, None, axis...  43 us
    ppermute x8, waiting for transfers between devices, with_halo(): lax.ppermute(lax.slice_in_dim(block, 0, width, axis=dim), axis, backward)  23.1 us
    another operation x100, local copies, waits for them, and re-layouts, kernel_grad(): return jnp.stack(kernel_taps).reshape(7, 7, grad_z.shape[2])  20.7 us
    ppermute x8, starting transfers between devices, with_halo(): lax.ppermute(lax.slice_in_dim(block, 0, width, axis=dim), axis, backward)  13 us
  transfers between devices with their start and end apart: 17, of which 6 were waited for; matrix products, arithmetic and copies ran while one was open for 8% of the time, Pallas kernels for 0%

commit v1 on v0

v1 whole, which is shorter than its diff:
```python
import functools
import math

import jax
import jax.numpy as jnp
from jax import lax
from jax.experimental import pallas as pl
from jax.experimental.pallas import tpu as pltpu
from jax.sharding import PartitionSpec as P

EPSILON = 1e-06
ROOT_HALF = 0.7071067811865476
INV_ROOT_TAU = 0.3989422804014327
MESH = pl.DeviceIdType.MESH
F32 = jnp.float32
BF16 = jnp.bfloat16

C = 384
HID = 1536
TILE = 16
PIX = TILE * TILE
PITCH = 32
PROWS = TILE + 6
GROUPS = C // 128
CHUNK = 256
SMALL = 64
DIRS = tuple((dr, dc) for dr in (-1, 0, 1) for dc in (-1, 0, 1) if (dr, dc) != (0, 0))
TN = (((0,), (0,)), ((), ()))
NT = (((1,), (1,)), ((), ()))


def lanes(g):
    return pl.ds(g * 128, 128)


def gelu_parts(pre):
    cdf = 0.5 * (1.0 + lax.erf(pre * ROOT_HALF))
    density = jnp.exp(-0.5 * pre * pre) * INV_ROOT_TAU
    return pre * cdf, cdf + pre * density


def pad_row(i):
    return (i + 3) * PITCH + 8


def conv_into(src, kern, layer, flip, emit):
    block = 4

    def step(it, carry):
        g = it // (TILE // block)
        row = (it % (TILE // block)) * block
        col = pl.ds(pl.multiple_of(g * 128, 128), 128)
        acc = [[None, None] for _ in range(block)]
        for rho in range(block + 6):
            taps = [
                src[g, pl.ds((row + rho) * PITCH + 5 + s, 8, stride=2), :] for s in range(8)
            ]
            for i in range(block):
                a = rho - i
                if a < 0 or a > 6:
                    continue
                for b in range(7):
                    ka, kb = (6 - a, 6 - b) if flip else (a, b)
                    w = kern[layer, ka, pl.ds(kb, 1), col]
                    for par in range(2):
                        term = taps[b + par] * w
                        acc[i][par] = term if acc[i][par] is None else acc[i][par] + term
        for i in range(block):
            for par in range(2):
                emit(g, row + i, par, acc[i][par])
        return carry

    lax.fori_loop(0, GROUPS * (TILE // block), step, 0)


def taps_grad(grad, src, small, layer):
    def step(it, carry):
        g = it // 7
        a = it % 7
        col = pl.ds(pl.multiple_of(g * 128, 128), 128)
        acc = [None] * 7
        for i in range(TILE):
            dz = [grad[g, pl.ds(pad_row(i) + par, 8, stride=2), :] for par in range(2)]
            row = [src[g, pl.ds((i + a) * PITCH + 5 + s, 8, stride=2), :] for s in range(8)]
            for b in range(7):
                term = dz[0] * row[b] + dz[1] * row[b + 1]
                acc[b] = term if acc[b] is None else acc[b] + term
        rows = [jnp.sum(acc[b], axis=0, keepdims=True) for b in range(7)]
        rows.append(jnp.zeros((1, 128), F32))
        small[layer, pl.ds(pl.multiple_of(a * 8, 8), 8), col] = jnp.concatenate(rows, axis=0)
        return carry

    lax.fori_loop(0, GROUPS * 7, step, 0)


def kernel(
    act_ref,
    gout_ref,
    kern_ref,
    gain_ref,
    shift_ref,
    win_hbm,
    bin_ref,
    wout_hbm,
    gin_ref,
    gk_ref,
    gg_ref,
    gs_ref,
    gb_ref,
    gwi_ref,
    gwo_ref,
    win,
    wout,
    pads,
    z_ref,
    hat_ref,
    inv_ref,
    hid_ref,
    gn_ref,
    slope_ref,
    ga_ref,
    pre_ref,
    dn_ref,
    db_ref,
    red_ref,
    hsend,
    hrecv,
    csend,
    crecv,
    s1,
    r1,
    own1,
    s2,
    r2,
    own2,
    s3,
    r3,
    fsend,
    frecv,
    small,
    smc,
    smt,
    sma,
    smb,
    smz,
    smg,
    smx,
    wsem,
    hs,
    hr,
    cs,
    cr,
    p1s,
    p1r,
    p2s,
    p2r,
    p3s,
    p3r,
    fs,
    fr,
    mcs,
    mcr,
    mas,
    mar,
    mbs,
    mbr,
    mzs,
    mzr,
    mgs,
    mgr,
    mxs,
    mxr,
):
    r = lax.axis_index("rows")
    c = lax.axis_index("cols")
    y, zl = r // 4, r % 4
    x, zh, core = c // 4, (c // 2) % 2, c % 2
    z = zh * 4 + zl
    first = y * (1 - core) + x * core
    second = x * (1 - core) + y * core
    scale = 1.0 / math.sqrt(256 * 256)

    def device(dx, dy, dz, dcore):
        return (dy * 4 + dz % 4, dx * 4 + (dz // 4) * 2 + dcore)

    def first_peer(k):
        q = (first + k) % 4
        return device(x * (1 - core) + q * core, q * (1 - core) + y * core, z, core)

    def second_peer(k):
        q = (second + k) % 4
        return device(q * (1 - core) + x * core, y * (1 - core) + q * core, z, core)

    def z_peer(k):
        return device(x, y, (z + k) % 8, core)

    def last_target(q):
        return device(q // 2, first, (q % 2) * 4 + second, core)

    def last_source(zs):
        return device(zl * (1 - core) + y * core, y * (1 - core) + zl * core, zs, core)

    partner = (r, c + 1 - 2 * core)

    def is_me(dev):
        return jnp.logical_and(dev[0] == r, dev[1] == c)

    def exists(d):
        rr, cc = r + d[0], c + d[1]
        return jnp.logical_and(
            jnp.logical_and(rr >= 0, rr < 16), jnp.logical_and(cc >= 0, cc < 16)
        )

    barrier = pltpu.get_barrier_semaphore()

    def greet(dev):
        pl.semaphore_signal(barrier, inc=1, device_id=dev, device_id_type=MESH)

    count = jnp.int32(13)
    for d in DIRS:
        ok = exists(d)

        @pl.when(ok)
        def _(d=d):
            greet((r + d[0], c + d[1]))

        count = count + ok.astype(jnp.int32)
    for k in range(1, 4):
        greet(first_peer(k))
        greet(second_peer(k))
    for k in range(1, 8):
        greet(z_peer(k))
    for q in range(8):
        for dev in (last_target(q), last_source(q)):
            away = jnp.logical_not(is_me(dev))

            @pl.when(away)
            def _(dev=dev):
                greet(dev)

            count = count + away.astype(jnp.int32)

    weight_copies = []
    for n, (src, dst, l) in enumerate(
        ((win_hbm, win, 0), (wout_hbm, wout, 0), (win_hbm, win, 1), (wout_hbm, wout, 1))
    ):
        copy = pltpu.make_async_copy(src.at[l], dst.at[l], wsem.at[n])
        copy.start()
        weight_copies.append(copy)

    zero = jnp.zeros((PITCH, 128), F32)

    def clear(it, carry):
        for p in range(4):
            for g in range(GROUPS):
                pads[p, g, pl.ds(pl.multiple_of(it * PITCH, PITCH), PITCH), :] = zero
        return carry

    lax.fori_loop(0, PROWS, clear, 0)

    def fill(it, carry):
        rows = pl.ds(pl.multiple_of(it * TILE, TILE), TILE)
        for g in range(GROUPS):
            pads[0, g, pl.ds(pl.multiple_of(pad_row(it), 8), TILE), :] = act_ref[
                rows, lanes(g)
            ].astype(F32)
        gn_ref[1, 1, rows, :] = gout_ref[rows, :]
        return carry

    lax.fori_loop(0, TILE, fill, 0)

    def halo_copy(e, n):
        d = DIRS[n]
        size = 32 if d[0] != 0 and d[1] != 0 else 48
        return pltpu.make_async_remote_copy(
            src_ref=hsend.at[e, n, pl.ds(0, size)],
            dst_ref=hrecv.at[e, 7 - n, pl.ds(0, size)],
            send_sem=hs.at[e, n],
            recv_sem=hr.at[e, 7 - n],
            device_id=(r + d[0], c + d[1]),
            device_id_type=MESH,
        )

    def halo_start(e, p):
        for n, d in enumerate(DIRS):
            row0 = {-1: 0, 0: 0, 1: TILE - 3}[d[0]]
            for g in range(GROUPS):
                if d[1] == 0:
                    for k in range(3):
                        hsend[e, n, pl.ds(k * 16, 16), lanes(g)] = pads[
                            p, g, pl.ds(pad_row(row0 + k), TILE), :
                        ].astype(BF16)
                elif d[0] == 0:
                    col0 = 0 if d[1] < 0 else TILE - 3
                    for k in range(3):
                        hsend[e, n, pl.ds(k * 16, 16), lanes(g)] = pads[
                            p, g, pl.ds(pad_row(0) + col0 + k, TILE, stride=PITCH), :
                        ].astype(BF16)
                else:
                    col0 = 0 if d[1] < 0 else 8
                    parts = [
                        pads[p, g, pl.ds(pad_row(row0 + k) + col0, 8), :] for k in range(3)
                    ]
                    hsend[e, n, pl.ds(0, 32), lanes(g)] = jnp.concatenate(
                        parts + [parts[2]], axis=0
                    ).astype(BF16)

            @pl.when(exists(d))
            def _(n=n):
                halo_copy(e, n).start()

    def halo_finish(e, p):
        for n, d in enumerate(DIRS):

            @pl.when(exists(d))
            def _(n=n, d=d):
                copy = halo_copy(e, n)
                copy.wait_send()
                size = 32 if d[0] != 0 and d[1] != 0 else 48
                pltpu.make_async_remote_copy(
                    src_ref=hsend.at[e, n, pl.ds(0, size)],
                    dst_ref=hrecv.at[e, n, pl.ds(0, size)],
                    send_sem=hs.at[e, n],
                    recv_sem=hr.at[e, n],
                    device_id=(r + d[0], c + d[1]),
                    device_id_type=MESH,
                ).wait_recv()
                row0 = {-1: -3, 0: 0, 1: TILE}[d[0]]
                for g in range(GROUPS):
                    got = hrecv[e, n, pl.ds(0, size), lanes(g)].astype(F32)
                    if d[1] == 0:
                        for k in range(3):
                            pads[p, g, pl.ds(pad_row(row0 + k), TILE), :] = got[
                                k * 16 : k * 16 + 16
                            ]
                    elif d[0] == 0:
                        col0 = -3 if d[1] < 0 else TILE
                        for k in range(3):
                            pads[
                                p, g, pl.ds(pad_row(0) + col0 + k, TILE, stride=PITCH), :
                            ] = got[k * 16 : k * 16 + 16]
                    else:
                        col0 = -8 if d[1] < 0 else TILE
                        for k in range(3):
                            pads[p, g, pl.ds(pad_row(row0 + k) + col0, 8), :] = got[
                                k * 8 : k * 8 + 8
                            ]

    pl.semaphore_wait(barrier, count)
    halo_start(0, 0)

    def forward_norm(layer, p):
        def emit(g, i, par, value):
            z_ref[g, pl.ds(i * TILE + par, 8, stride=2), :] = value

        conv_into(pads.at[p], kern_ref, layer, False, emit)

        def step(it, carry):
            rows = pl.ds(pl.multiple_of(it * 32, 32), 32)
            zs = [z_ref[g, rows, :] for g in range(GROUPS)]
            mean = jnp.sum(zs[0] + zs[1] + zs[2], axis=-1, keepdims=True) * (1.0 / C)
            cen = [v - mean for v in zs]
            var = jnp.sum(
                cen[0] * cen[0] + cen[1] * cen[1] + cen[2] * cen[2], axis=-1, keepdims=True
            ) * (1.0 / C)
            inv = lax.rsqrt(var + EPSILON)
            inv_ref[layer, rows, :] = jnp.broadcast_to(inv, (32, 128))
            for g in range(GROUPS):
                hat = cen[g] * inv
                hat_ref[layer, g, rows, :] = hat
                gn_ref[layer, 0, rows, lanes(g)] = (
                    hat * gain_ref[pl.ds(layer, 1), lanes(g)]
                    + shift_ref[pl.ds(layer, 1), lanes(g)]
                ).astype(BF16)
            return carry

        lax.fori_loop(0, PIX // 32, step, 0)

    def hidden_forward(layer):
        def step(n, carry):
            cols = pl.ds(pl.multiple_of(n * CHUNK, CHUNK), CHUNK)
            pre_ref[...] = jnp.dot(
                gn_ref[layer, 0], win[layer, :, cols], preferred_element_type=F32
            )
            bias = bin_ref[pl.ds(layer, 1), cols]

            def inner(it, carry):
                rows = pl.ds(pl.multiple_of(it * 32, 32), 32)
                act, slope = gelu_parts(pre_ref[rows, :] + bias)
                hid_ref[layer, 1, rows, cols] = act.astype(BF16)
                slope_ref[layer, rows, cols] = slope
                return carry

            lax.fori_loop(0, PIX // 32, inner, 0)
            return carry

        lax.fori_loop(0, HID // CHUNK, step, 0)

    def hidden_grad(layer):
        def step(n, carry):
            cols = pl.ds(pl.multiple_of(n * CHUNK, CHUNK), CHUNK)
            ga_ref[:, cols] = jnp.dot(
                gn_ref[layer, 1], wout[layer, :, cols], preferred_element_type=F32
            )
            return carry

        lax.fori_loop(0, HID // CHUNK, step, 0)

    def slope_times(layer):
        def step(n, carry):
            cols = pl.ds(pl.multiple_of(n * CHUNK, CHUNK), CHUNK)

            def inner(it, total):
                rows = pl.ds(pl.multiple_of(it * 32, 32), 32)
                grad = ga_ref[rows, cols] * slope_ref[layer, rows, cols]
                hid_ref[layer, 0, rows, cols] = grad.astype(BF16)
                return total + (grad[0:8] + grad[8:16]) + (grad[16:24] + grad[24:32])

            total = lax.fori_loop(0, PIX // 32, inner, jnp.zeros((8, CHUNK), F32))
            db_ref[pl.ds(layer, 1), cols] = jnp.sum(total, axis=0, keepdims=True)
            return carry

        lax.fori_loop(0, HID // CHUNK, step, 0)

    def norm_grad(layer, p):
        dn_ref[...] = lax.dot_general(
            hid_ref[layer, 0], win[layer], NT, preferred_element_type=F32
        )
        red_ref[...] = jnp.zeros_like(red_ref)

        def step(it, carry):
            rows = pl.ds(pl.multiple_of(it * 32, 32), 32)
            dn = [dn_ref[rows, lanes(g)] for g in range(GROUPS)]
            hat = [hat_ref[layer, g, rows, :] for g in range(GROUPS)]
            sc = [dn[g] * gain_ref[pl.ds(layer, 1), lanes(g)] for g in range(GROUPS)]
            m1 = jnp.sum(sc[0] + sc[1] + sc[2], axis=-1, keepdims=True) * (1.0 / C)
            m2 = jnp.sum(
                sc[0] * hat[0] + sc[1] * hat[1] + sc[2] * hat[2], axis=-1, keepdims=True
            ) * (1.0 / C)
            inv = inv_ref[layer, rows, :]
            for g in range(GROUPS):
                dz = (inv * (sc[g] - m1 - hat[g] * m2)).astype(BF16).astype(F32)
                for k in range(2):
                    pads[
                        p, g, pl.ds(pl.multiple_of(pad_row(it * 2 + k), 8), TILE), :
                    ] = dz[k * TILE : (k + 1) * TILE]
                prod = dn[g] * hat[g]
                red_ref[0, :, lanes(g)] += (prod[0:8] + prod[8:16]) + (prod[16:24] + prod[24:32])
                red_ref[1, :, lanes(g)] += (dn[g][0:8] + dn[g][8:16]) + (
                    dn[g][16:24] + dn[g][24:32]
                )
            return carry

        lax.fori_loop(0, PIX // 32, step, 0)
        small[layer, pl.ds(56, 1), :] = jnp.sum(red_ref[0], axis=0, keepdims=True)
        small[layer, pl.ds(57, 1), :] = jnp.sum(red_ref[1], axis=0, keepdims=True)
        for k in range(4):
            small[layer, pl.ds(58 + k, 1), :] = db_ref[pl.ds(layer, 1), pl.ds(k * C, C)]
        small[layer, pl.ds(62, 2), :] = jnp.zeros((2, C), F32)

    def remote(src, dst, ssem, rsem, dev):
        return pltpu.make_async_remote_copy(
            src_ref=src,
            dst_ref=dst,
            send_sem=ssem,
            recv_sem=rsem,
            device_id=dev,
            device_id_type=MESH,
        )

    def pair_copy(l, q):
        return remote(csend.at[l, q], crecv.at[l, q], cs.at[l, q], cr.at[l, q], partner)

    def first_copy(l, k):
        return remote(
            s1.at[l, k - 1], r1.at[l, k - 1], p1s.at[l, k - 1], p1r.at[l, k - 1], first_peer(k)
        )

    def second_copy(l, k):
        return remote(
            s2.at[l, k - 1], r2.at[l, k - 1], p2s.at[l, k - 1], p2r.at[l, k - 1], second_peer(k)
        )

    def last_copy(l, q):
        return remote(s3.at[l, q], r3.at[l, z], p3s.at[l, q], p3r.at[l, z], last_target(q))

    def back_copy(l):
        return remote(fsend.at[l], frecv.at[l], fs.at[l], fr.at[l], partner)

    def weight_grad(l, m, q):
        return lax.dot_general(
            hid_ref[l, m, :, pl.ds(pl.multiple_of(q * C, C), C)],
            gn_ref[l, m],
            TN,
            preferred_element_type=F32,
        )

    def reduce_start(l):
        def away(q, carry):
            csend[l, q] = weight_grad(l, 1 - core, q).astype(BF16)
            pair_copy(l, q).start()
            return carry

        lax.fori_loop(0, 4, away, 0)

    def reduce_first(l):
        def block(k):
            q = (first + k) % 4
            mine = weight_grad(l, core, q)
            pair_copy(l, q).wait()
            return mine + crecv[l, q].astype(F32)

        def step(k, carry):
            s1[l, k - 1] = block(k).astype(BF16)
            first_copy(l, k).start()
            return carry

        lax.fori_loop(1, 4, step, 0)
        own1[...] = block(0)

    def reduce_second(l):
        for k in range(1, 4):
            first_copy(l, k).wait()

        def block(k):
            rows = pl.ds(pl.multiple_of(((second + k) % 4) * 96, 96), 96)
            return (
                own1[rows, :]
                + r1[l, 0, rows, :].astype(F32)
                + r1[l, 1, rows, :].astype(F32)
                + r1[l, 2, rows, :].astype(F32)
            )

        def step(k, carry):
            s2[l, k - 1] = block(k).astype(BF16)
            second_copy(l, k).start()
            return carry

        lax.fori_loop(1, 4, step, 0)
        own2[...] = block(0)

    def reduce_last(l):
        for k in range(1, 4):
            second_copy(l, k).wait()
        total = (
            own2[...]
            + r2[l, 0].astype(F32)
            + r2[l, 1].astype(F32)
            + r2[l, 2].astype(F32)
        )
        pad = jnp.zeros((4, C), F32)
        for q in range(8):
            s3[l, q] = jnp.concatenate([total[12 * q : 12 * q + 12], pad], axis=0).astype(BF16)
            me = is_me(last_target(q))

            @pl.when(jnp.logical_not(me))
            def _(q=q):
                last_copy(l, q).start()

            @pl.when(me)
            def _(q=q):
                r3[l, z] = s3[l, q]

    def reduce_back(l):
        for q in range(8):

            @pl.when(jnp.logical_not(is_me(last_target(q))))
            def _(q=q):
                last_copy(l, q).wait_send()

            @pl.when(jnp.logical_not(is_me(last_source(q))))
            def _(q=q):
                remote(
                    s3.at[l, 0], r3.at[l, q], p3s.at[l, 0], p3r.at[l, q], last_source(q)
                ).wait_recv()

        total = r3[l, 0].astype(F32)
        for q in range(1, 8):
            total = total + r3[l, q].astype(F32)
        total = total * scale
        pad = jnp.zeros((2, C), F32)
        low = jnp.concatenate([total[0:6], pad], axis=0)
        high = jnp.concatenate([total[6:12], pad], axis=0)
        zeroth = core == 0
        fsend[l] = jnp.where(zeroth, high, low)
        back_copy(l).start()
        return jnp.where(zeroth, low, high)

    def reduce_end(l, mine):
        back_copy(l).wait()
        other = frecv[l]
        zeroth = core == 0
        gwi_ref[l] = jnp.where(zeroth, mine, other)
        gwo_ref[l] = jnp.where(zeroth, other, mine)

    def small_pair(l):
        half = pl.ds(pl.multiple_of((1 - core) * 32, 32), 32)
        return remote(small.at[l, half], smc.at[l], mcs.at[l], mcr.at[l], partner)

    def small_first(l, k):
        q = (first + k) % 4
        return remote(
            smt.at[l, q], sma.at[l, k - 1], mas.at[l, k - 1], mar.at[l, k - 1], first_peer(k)
        )

    def small_second(l, k):
        return remote(
            smb.at[l, second],
            smb.at[l, second],
            mbs.at[l, k - 1],
            mbr.at[l, k - 1],
            second_peer(k),
        )

    def small_z(l, k):
        return remote(
            smz.at[l, z], smz.at[l, z], mzs.at[l, k - 1], mzr.at[l, k - 1], z_peer(k)
        )

    def small_gather(l, k):
        return remote(
            smg.at[l, first], smg.at[l, first], mgs.at[l, k - 1], mgr.at[l, k - 1], first_peer(k)
        )

    def small_back(l):
        return remote(smg.at[l], smx.at[l], mxs.at[l], mxr.at[l], partner)

    def small_0(l):
        small_pair(l).start()

    def small_1(l):
        small_pair(l).wait()
        for q in range(4):
            rows = pl.ds(pl.multiple_of(core * 32 + q * 8, 8), 8)
            smt[l, q] = small[l, rows, :] + smc[l, pl.ds(q * 8, 8), :]
        for k in range(1, 4):
            small_first(l, k).start()

    def small_2(l):
        for k in range(1, 4):
            small_first(l, k).wait()
        smb[l, second] = (smt[l, first] + sma[l, 0]) + (sma[l, 1] + sma[l, 2])
        for k in range(1, 4):
            small_second(l, k).start()

    def small_3(l):
        for k in range(1, 4):
            small_second(l, k).wait()
        smz[l, z] = (smb[l, 0] + smb[l, 1]) + (smb[l, 2] + smb[l, 3])
        for k in range(1, 8):
            small_z(l, k).start()

    def small_4(l):
        for k in range(1, 8):
            small_z(l, k).wait()
        total = smz[l, 0]
        for q in range(1, 8):
            total = total + smz[l, q]
        smg[l, first] = total * scale
        for k in range(1, 4):
            small_gather(l, k).start()

    def small_5(l):
        for k in range(1, 4):
            small_gather(l, k).wait()
        small_back(l).start()

    def small_6(l):
        small_back(l).wait()
        zeroth = core == 0
        low = [jnp.where(zeroth, smg[l, q], smx[l, q]) for q in range(4)]
        high = [jnp.where(zeroth, smx[l, q], smg[l, q]) for q in range(4)]
        full = jnp.concatenate(low + high, axis=0)
        for a in range(7):
            gk_ref[l, a] = full[a * 8 : a * 8 + 7]
        gg_ref[pl.ds(l, 1), :] = full[56:57]
        gs_ref[pl.ds(l, 1), :] = full[57:58]
        for k in range(4):
            gb_ref[pl.ds(l, 1), pl.ds(k * C, C)] = full[58 + k : 59 + k]

    for copy in weight_copies:
        copy.wait()
    hidden_grad(1)
    halo_finish(0, 0)
    forward_norm(0, 0)
    hidden_forward(0)
    dn_ref[...] = lax.dot_general(hid_ref[0, 1], wout[0], NT, preferred_element_type=F32)

    def to_middle(it, carry):
        rows = pl.ds(pl.multiple_of(it * TILE, TILE), TILE)
        at = pl.ds(pl.multiple_of(pad_row(it), 8), TILE)
        for g in range(GROUPS):
            pads[1, g, at, :] = (pads[0, g, at, :] + dn_ref[rows, lanes(g)]).astype(BF16).astype(F32)
        return carry

    lax.fori_loop(0, TILE, to_middle, 0)
    halo_start(1, 1)
    halo_finish(1, 1)
    forward_norm(1, 1)
    hidden_forward(1)
    slope_times(1)
    norm_grad(1, 2)
    halo_start(2, 2)
    reduce_start(1)
    taps_grad(pads.at[2], pads.at[1], small, 1)
    small_0(1)
    reduce_first(1)
    halo_finish(2, 2)

    def emit_mid(g, i, par, value):
        z_ref[g, pl.ds(i * TILE + par, 8, stride=2), :] = value

    conv_into(pads.at[2], kern_ref, 1, True, emit_mid)

    def to_grad_mid(it, carry):
        rows = pl.ds(pl.multiple_of(it * 32, 32), 32)
        for g in range(GROUPS):
            gn_ref[0, 1, rows, lanes(g)] = (
                gn_ref[1, 1, rows, lanes(g)].astype(F32) + z_ref[g, rows, :]
            ).astype(BF16)
        return carry

    lax.fori_loop(0, PIX // 32, to_grad_mid, 0)
    small_1(1)
    hidden_grad(0)
    slope_times(0)
    reduce_second(1)
    small_2(1)
    norm_grad(0, 3)
    halo_start(3, 3)
    reduce_start(0)
    reduce_last(1)
    small_3(1)
    reduce_first(0)
    mine_1 = reduce_back(1)
    small_4(1)
    taps_grad(pads.at[3], pads.at[0], small, 0)
    small_0(0)
    small_5(1)
    halo_finish(3, 3)
    small_1(0)
    conv_into(pads.at[3], kern_ref, 0, True, emit_mid)

    def to_grad_in(it, carry):
        rows = pl.ds(pl.multiple_of(it * 32, 32), 32)
        for g in range(GROUPS):
            gin_ref[rows, lanes(g)] = (
                gn_ref[0, 1, rows, lanes(g)].astype(F32) + z_ref[g, rows, :]
            ).astype(BF16)
        return carry

    lax.fori_loop(0, PIX // 32, to_grad_in, 0)
    reduce_end(1, mine_1)
    small_6(1)
    small_2(0)
    small_3(0)
    reduce_second(0)
    small_4(0)
    reduce_last(0)
    small_5(0)
    mine_0 = reduce_back(0)
    small_6(0)
    reduce_end(0, mine_0)


def shards(activations, grad_out, kernels, norm_gains, norm_shifts, w_in, b_in, w_out):
    vmem = pl.BlockSpec(memory_space=pltpu.VMEM)
    hbm = pl.BlockSpec(memory_space=pl.ANY)
    dma = pltpu.SemaphoreType.DMA
    pad_size = PROWS * PITCH
    scratch = [
        pltpu.VMEM((2, C, HID), BF16),
        pltpu.VMEM((2, C, HID), BF16),
        pltpu.VMEM((4, GROUPS, pad_size, 128), F32),
        pltpu.VMEM((GROUPS, PIX, 128), F32),
        pltpu.VMEM((2, GROUPS, PIX, 128), F32),
        pltpu.VMEM((2, PIX, 128), F32),
        pltpu.VMEM((2, 2, PIX, HID), BF16),
        pltpu.VMEM((2, 2, PIX, C), BF16),
        pltpu.VMEM((2, PIX, HID), F32),
        pltpu.VMEM((PIX, HID), F32),
        pltpu.VMEM((PIX, CHUNK), F32),
        pltpu.VMEM((PIX, C), F32),
        pltpu.VMEM((2, HID), F32),
        pltpu.VMEM((2, 8, C), F32),
        pltpu.VMEM((4, 8, 48, C), BF16),
        pltpu.VMEM((4, 8, 48, C), BF16),
        pltpu.VMEM((2, 4, C, C), BF16),
        pltpu.VMEM((2, 4, C, C), BF16),
        pltpu.VMEM((2, 3, C, C), BF16),
        pltpu.VMEM((2, 3, C, C), BF16),
        pltpu.VMEM((C, C), F32),
        pltpu.VMEM((2, 3, 96, C), BF16),
        pltpu.VMEM((2, 3, 96, C), BF16),
        pltpu.VMEM((96, C), F32),
        pltpu.VMEM((2, 8, 16, C), BF16),
        pltpu.VMEM((2, 8, 16, C), BF16),
        pltpu.VMEM((2, 8, C), F32),
        pltpu.VMEM((2, 8, C), F32),
        pltpu.VMEM((2, SMALL, C), F32),
        pltpu.VMEM((2, 32, C), F32),
        pltpu.VMEM((2, 4, 8, C), F32),
        pltpu.VMEM((2, 3, 8, C), F32),
        pltpu.VMEM((2, 4, 8, C), F32),
        pltpu.VMEM((2, 8, 8, C), F32),
        pltpu.VMEM((2, 4, 8, C), F32),
        pltpu.VMEM((2, 4, 8, C), F32),
        dma((4,)),
        dma((4, 8)),
        dma((4, 8)),
        dma((2, 4)),
        dma((2, 4)),
        dma((2, 3)),
        dma((2, 3)),
        dma((2, 3)),
        dma((2, 3)),
        dma((2, 8)),
        dma((2, 8)),
        dma((2,)),
        dma((2,)),
        dma((2,)),
        dma((2,)),
        dma((2, 3)),
        dma((2, 3)),
        dma((2, 3)),
        dma((2, 3)),
        dma((2, 7)),
        dma((2, 7)),
        dma((2, 3)),
        dma((2, 3)),
        dma((2,)),
        dma((2,)),
    ]
    sds = jax.ShapeDtypeStruct
    outs = pl.pallas_call(
        kernel,
        out_shape=(
            sds((PIX, C), BF16),
            sds((2, 7, 7, C), F32),
            sds((2, C), F32),
            sds((2, C), F32),
            sds((2, HID), F32),
            sds((2, 8, C), F32),
            sds((2, 8, C), F32),
        ),
        in_specs=[vmem, vmem, vmem, vmem, vmem, hbm, vmem, hbm],
        out_specs=(vmem,) * 7,
        scratch_shapes=scratch,
        compiler_params=pltpu.CompilerParams(
            collective_id=0, has_side_effects=True, vmem_limit_bytes=64000000
        ),
        name="convnext_step",
    )(
        activations.reshape(PIX, C),
        grad_out.reshape(PIX, C),
        kernels,
        norm_gains,
        norm_shifts,
        w_in,
        b_in,
        w_out,
    )
    grad_in, gk, gg, gs, gb, gwi, gwo = outs
    return (
        grad_in.reshape(activations.shape),
        gk,
        gg,
        gs,
        gb,
        jnp.swapaxes(gwi[:, :6], 1, 2),
        jnp.swapaxes(gwo[:, :6], 1, 2),
    )


def solution(mesh):
    return jax.shard_map(
        shards,
        mesh=mesh,
        in_specs=(P("rows", "cols", None), P("rows", "cols", None), P(), P(), P(), P(), P(), P()),
        out_specs=(
            P("rows", "cols", None),
            P(),
            P(),
            P(),
            P(),
            P(None, None, ("rows", "cols")),
            P(None, None, ("rows", "cols")),
        ),
        check_vma=False,
    )
```

time: 463 us -> 106 us (0.23)
  waiting for transfers between devices: 200 us -> 0 us
  Pallas kernels: 0 us -> 94.8 us
  blocking collectives: 84.4 us -> 0 us
  starting transfers between devices: 56.1 us -> 0 us
  local copies, waits for them, and re-layouts: 53.2 us -> 10.7 us
  other arithmetic: 34.6 us -> 0 us
  between operations: 16.8 us -> 0.64 us
  matrix products: 14.8 us -> 0 us
    psum x1 -> x0, waiting for transfers between devices: 177 us -> none  [shards(): lax.psum((jnp.stack([back_one[1], back_two[1]]) * grad_scale, jnp.stack([...]
    pallas_call x0 -> x1, Pallas kernels: none -> 94.8 us  [shards(): pl.pallas_call(kernel, out_shape=(sds((PIX, C), BF16), sds((2, 7, 7, C),...]
    psum x1 -> x0, blocking collectives: 84.4 us -> none  [shards(): lax.psum((jnp.stack([back_one[1], back_two[1]]) * grad_scale, jnp.stack([...]
    ppermute x16 -> x0, starting transfers between devices: 56 us -> none  [the longest x8 43 us: with_halo(): lax.ppermute(lax.slice_in_dim(block, block.shape[dim] - width, None, axis...]
    another operation x108 -> x0, local copies, waits for them, and re-layouts: 23.5 us -> none  [the longest x100 20.7 us: kernel_grad(): return jnp.stack(kernel_taps).reshape(7, 7, grad_z.shape[2])]
    ppermute x16 -> x0, waiting for transfers between devices: 23.1 us -> none  [the longest x8 23.1 us: with_halo(): lax.ppermute(lax.slice_in_dim(block, 0, width, axis=dim), axis, backward)]
    mul x2 -> x0, local copies, waits for them, and re-layouts: 16.3 us -> none  [the longest x1 8.17 us: shards(): stacked_in = jnp.stack([back_one[5], back_two[5]]) * grad_scale]
    dot_general x11 -> x0, matrix products: 14.8 us -> none  [the longest x2 3.89 us: layer_back(): lax.dot_general(grad_flat, act_b, (((0,), (0,)), ((), ())), preferred_ele...]
  transfers between devices with their start and end apart: 17 -> 0, of which waited for: 6 -> 0; matrix products, arithmetic and copies ran while one was open for 8% -> 0% of each run, Pallas kernels for 0% -> 0%
where the time goes in v1:
time: 106 us
  Pallas kernels  94.8 us (89%)
  local copies, waits for them, and re-layouts  10.7 us (10%)
    pallas_call x1, Pallas kernels, shards(): pl.pallas_call(kernel, out_shape=(sds((PIX, C), BF16), sds((2, 7, 7, C),...  94.8 us
    unnamed x8, local copies, waits for them, and re-layouts  9.93 us

profile of v1, /device:TPU:1, one launch (start us, length us, event | category | flops | bytes accessed | tf_op | source)
XLA Modules:
  0.0 106.1 jit_solution(7004374113068278327)
XLA Ops:
  0.6 1.6 %copy.15.kern_ref = f32[2,7,7,384]{3,2,1,0:T(8,128)} copy(f32[2,7,7,384]{3,0,2,1:T(2,128)} %param.10) | data formatting | bytes 301056 | tf_op args[2]
  2.2 94.8 %convnext_step.1 = (bf16[256,384]{1,0:T(8,128)(2,1)}, f32[2,7,7,384]{3,2,1,0:T(8,128)}, f32[2,384]{1,0:T(2,128)}, f32[2,384]{1,0:T(2,128)}, f32[2,1536]{1,0:T(2,...) custom-call(bf16[256,384]{1,0:T(8,128)(2,1)} %bitcast.7, bf16[256,384]{1,0:T(8,128)(2,1)} %bitcast.8, ...), custom_call_target="tpu_custom_call" | custom-call | tf_op jit(solution)/shard_map/convnext_step/pallas_call | solution.py:835
  97.0 0.8 slice_bitcast_fusion
  97.8 0.6 copy.17
  98.4 0.6 copy.18
  99.0 1.7 %copy.16 = f32[2,7,7,384]{3,0,2,1:T(2,128)} copy(f32[2,7,7,384]{3,2,1,0:T(8,128)} %get-tuple-element.22) | data formatting | bytes 301056
  100.7 1.6 %copy.23 = bf16[16,16,384]{2,1,0:T(8,128)(2,1)} copy(bf16[16,16,384]{2,1,0:T(8,128)(2,1)} %bitcast.9) | data formatting | bytes 393216
  102.3 1.3 %copy.24 = f32[2,384]{1,0:T(2,128)} copy(f32[2,384]{1,0:T(2,128)} %get-tuple-element.39) | data formatting | bytes 6144
  103.5 1.3 %copy.25 = f32[2,384]{1,0:T(2,128)} copy(f32[2,384]{1,0:T(2,128)} %get-tuple-element.40) | data formatting | bytes 6144
  104.8 1.3 %copy.26 = f32[2,1536]{1,0:T(2,128)} copy(f32[2,1536]{1,0:T(2,128)} %get-tuple-element.41) | data formatting | bytes 24576

commit v2 on v1

--- a/solution.py
+++ b/solution.py
@@ -61,7 +61,7 @@
                     continue
                 for b in range(7):
                     ka, kb = (6 - a, 6 - b) if flip else (a, b)
-                    w = kern[layer, ka, pl.ds(kb, 1), col]
+                    w = kern[ka, kb, pl.ds(layer, 1), col]
                     for par in range(2):
                         term = taps[b + par] * w
                         acc[i][par] = term if acc[i][par] is None else acc[i][par] + term
@@ -94,9 +94,9 @@
 
 
 def kernel(
-    act_ref,
-    gout_ref,
-    kern_ref,
+    act_hbm,
+    gout_hbm,
+    kern_hbm,
     gain_ref,
     shift_ref,
     win_hbm,
@@ -109,6 +109,8 @@
     gb_ref,
     gwi_ref,
     gwo_ref,
+    act_ref,
+    kern_ref,
     win,
     wout,
     pads,
@@ -127,6 +129,8 @@
     hrecv,
     csend,
     crecv,
+    s0,
+    r0,
     s1,
     r1,
     own1,
@@ -150,6 +154,8 @@
     hr,
     cs,
     cr,
+    p0s,
+    p0r,
     p1s,
     p1r,
     p2s,
@@ -211,6 +217,13 @@
             jnp.logical_and(rr >= 0, rr < 16), jnp.logical_and(cc >= 0, cc < 16)
         )
 
+    act_copy = pltpu.make_async_copy(act_hbm, act_ref, wsem.at[4])
+    act_copy.start()
+    kern_copy = pltpu.make_async_copy(kern_hbm, kern_ref, wsem.at[5])
+    gout_copy = pltpu.make_async_copy(gout_hbm, gn_ref.at[1, 1], wsem.at[6])
+    kern_copy.start()
+    gout_copy.start()
+
     barrier = pltpu.get_barrier_semaphore()
 
     def greet(dev):
@@ -257,6 +270,7 @@
         return carry
 
     lax.fori_loop(0, PROWS, clear, 0)
+    act_copy.wait()
 
     def fill(it, carry):
         rows = pl.ds(pl.multiple_of(it * TILE, TILE), TILE)
@@ -264,7 +278,6 @@
             pads[0, g, pl.ds(pl.multiple_of(pad_row(it), 8), TILE), :] = act_ref[
                 rows, lanes(g)
             ].astype(F32)
-        gn_ref[1, 1, rows, :] = gout_ref[rows, :]
         return carry
 
     lax.fori_loop(0, TILE, fill, 0)
@@ -314,8 +327,6 @@
 
             @pl.when(exists(d))
             def _(n=n, d=d):
-                copy = halo_copy(e, n)
-                copy.wait_send()
                 size = 32 if d[0] != 0 and d[1] != 0 else 48
                 pltpu.make_async_remote_copy(
                     src_ref=hsend.at[e, n, pl.ds(0, size)],
@@ -348,6 +359,7 @@
 
     pl.semaphore_wait(barrier, count)
     halo_start(0, 0)
+    kern_copy.wait()
 
     def forward_norm(layer, p):
         def emit(g, i, par, value):
@@ -471,10 +483,13 @@
     def pair_copy(l, q):
         return remote(csend.at[l, q], crecv.at[l, q], cs.at[l, q], cr.at[l, q], partner)
 
+    def relay_copy(l, k):
+        return remote(
+            s0.at[l, pl.ds(192 * k, 192)], r0.at[l, k], p0s.at[l, k], p0r.at[l, k], first_peer(1 + 2 * k)
+        )
+
     def first_copy(l, k):
-        return remote(
-            s1.at[l, k - 1], r1.at[l, k - 1], p1s.at[l, k - 1], p1r.at[l, k - 1], first_peer(k)
-        )
+        return remote(s1.at[l, k], r1.at[l, k], p1s.at[l, k], p1r.at[l, k], first_peer(1 + 2 * k))
 
     def second_copy(l, k):
         return remote(
@@ -503,32 +518,44 @@
 
         lax.fori_loop(0, 4, away, 0)
 
+    def pair_block(l, k):
+        q = (first + k) % 4
+        mine = weight_grad(l, core, q)
+        pair_copy(l, q).wait_recv()
+        return mine + crecv[l, q].astype(F32)
+
+    def reduce_relay(l):
+        s0[l] = pair_block(l, 2).astype(BF16)
+        for k in range(2):
+            relay_copy(l, k).start()
+
+    def reduce_pair(l):
+        def step(i, carry):
+            own1[l, i] = pair_block(l, 1 + 2 * i)
+            return carry
+
+        lax.fori_loop(0, 2, step, 0)
+        own1[l, 2] = pair_block(l, 0)
+
     def reduce_first(l):
-        def block(k):
-            q = (first + k) % 4
-            mine = weight_grad(l, core, q)
-            pair_copy(l, q).wait()
-            return mine + crecv[l, q].astype(F32)
-
-        def step(k, carry):
-            s1[l, k - 1] = block(k).astype(BF16)
+        for k in range(2):
+            relay_copy(l, k).wait_recv()
+            part = pl.ds(192 * k, 192)
+            rest = pl.ds(192 * (1 - k), 192)
+            s1[l, k, part, :] = (own1[l, k, part, :] + r0[l, k].astype(F32)).astype(BF16)
+            s1[l, k, rest, :] = own1[l, k, rest, :].astype(BF16)
             first_copy(l, k).start()
-            return carry
-
-        lax.fori_loop(1, 4, step, 0)
-        own1[...] = block(0)
 
     def reduce_second(l):
-        for k in range(1, 4):
-            first_copy(l, k).wait()
+        for k in range(2):
+            first_copy(l, k).wait_recv()
 
         def block(k):
             rows = pl.ds(pl.multiple_of(((second + k) % 4) * 96, 96), 96)
             return (
-                own1[rows, :]
+                own1[l, 2, rows, :]
                 + r1[l, 0, rows, :].astype(F32)
                 + r1[l, 1, rows, :].astype(F32)
-                + r1[l, 2, rows, :].astype(F32)
             )
 
         def step(k, carry):
@@ -541,7 +568,7 @@
 
     def reduce_last(l):
         for k in range(1, 4):
-            second_copy(l, k).wait()
+            second_copy(l, k).wait_recv()
         total = (
             own2[...]
             + r2[l, 0].astype(F32)
@@ -563,10 +590,6 @@
 
     def reduce_back(l):
         for q in range(8):
-
-            @pl.when(jnp.logical_not(is_me(last_target(q))))
-            def _(q=q):
-                last_copy(l, q).wait_send()
 
             @pl.when(jnp.logical_not(is_me(last_source(q))))
             def _(q=q):
@@ -587,11 +610,14 @@
         return jnp.where(zeroth, low, high)
 
     def reduce_end(l, mine):
-        back_copy(l).wait()
+        back_copy(l).wait_recv()
         other = frecv[l]
         zeroth = core == 0
-        gwi_ref[l] = jnp.where(zeroth, mine, other)
-        gwo_ref[l] = jnp.where(zeroth, other, mine)
+        wi = jnp.where(zeroth, mine, other)
+        wo = jnp.where(zeroth, other, mine)
+        for j in range(6):
+            gwi_ref[j, pl.ds(l, 1), :] = wi[j : j + 1]
+            gwo_ref[j, pl.ds(l, 1), :] = wo[j : j + 1]
 
     def small_pair(l):
         half = pl.ds(pl.multiple_of((1 - core) * 32, 32), 32)
@@ -629,7 +655,7 @@
         small_pair(l).start()
 
     def small_1(l):
-        small_pair(l).wait()
+        small_pair(l).wait_recv()
         for q in range(4):
             rows = pl.ds(pl.multiple_of(core * 32 + q * 8, 8), 8)
             smt[l, q] = small[l, rows, :] + smc[l, pl.ds(q * 8, 8), :]
@@ -638,21 +664,21 @@
 
     def small_2(l):
         for k in range(1, 4):
-            small_first(l, k).wait()
+            small_first(l, k).wait_recv()
         smb[l, second] = (smt[l, first] + sma[l, 0]) + (sma[l, 1] + sma[l, 2])
         for k in range(1, 4):
             small_second(l, k).start()
 
     def small_3(l):
         for k in range(1, 4):
-            small_second(l, k).wait()
+            small_second(l, k).wait_recv()
         smz[l, z] = (smb[l, 0] + smb[l, 1]) + (smb[l, 2] + smb[l, 3])
         for k in range(1, 8):
             small_z(l, k).start()
 
     def small_4(l):
         for k in range(1, 8):
-            small_z(l, k).wait()
+            small_z(l, k).wait_recv()
         total = smz[l, 0]
         for q in range(1, 8):
             total = total + smz[l, q]
@@ -662,27 +688,27 @@
 
     def small_5(l):
         for k in range(1, 4):
-            small_gather(l, k).wait()
+            small_gather(l, k).wait_recv()
         small_back(l).start()
 
     def small_6(l):
-        small_back(l).wait()
+        small_back(l).wait_recv()
         zeroth = core == 0
         low = [jnp.where(zeroth, smg[l, q], smx[l, q]) for q in range(4)]
         high = [jnp.where(zeroth, smx[l, q], smg[l, q]) for q in range(4)]
         full = jnp.concatenate(low + high, axis=0)
         for a in range(7):
-            gk_ref[l, a] = full[a * 8 : a * 8 + 7]
+            for b in range(7):
+                gk_ref[a, b, pl.ds(l, 1), :] = full[a * 8 + b : a * 8 + b + 1]
         gg_ref[pl.ds(l, 1), :] = full[56:57]
         gs_ref[pl.ds(l, 1), :] = full[57:58]
         for k in range(4):
             gb_ref[pl.ds(l, 1), pl.ds(k * C, C)] = full[58 + k : 59 + k]
 
+    halo_finish(0, 0)
+    forward_norm(0, 0)
     for copy in weight_copies:
         copy.wait()
-    hidden_grad(1)
-    halo_finish(0, 0)
-    forward_norm(0, 0)
     hidden_forward(0)
     dn_ref[...] = lax.dot_general(hid_ref[0, 1], wout[0], NT, preferred_element_type=F32)
 
@@ -695,16 +721,20 @@
 
     lax.fori_loop(0, TILE, to_middle, 0)
     halo_start(1, 1)
+    gout_copy.wait()
+    hidden_grad(1)
     halo_finish(1, 1)
     forward_norm(1, 1)
     hidden_forward(1)
     slope_times(1)
     norm_grad(1, 2)
     halo_start(2, 2)
-    reduce_start(1)
     taps_grad(pads.at[2], pads.at[1], small, 1)
     small_0(1)
-    reduce_first(1)
+    reduce_start(1)
+    small_1(1)
+    reduce_relay(1)
+    reduce_pair(1)
     halo_finish(2, 2)
 
     def emit_mid(g, i, par, value):
@@ -721,24 +751,24 @@
         return carry
 
     lax.fori_loop(0, PIX // 32, to_grad_mid, 0)
-    small_1(1)
+    small_2(1)
+    reduce_first(1)
     hidden_grad(0)
     slope_times(0)
-    reduce_second(1)
-    small_2(1)
+    reduce_start(0)
     norm_grad(0, 3)
     halo_start(3, 3)
-    reduce_start(0)
-    reduce_last(1)
     small_3(1)
-    reduce_first(0)
-    mine_1 = reduce_back(1)
-    small_4(1)
+    reduce_relay(0)
     taps_grad(pads.at[3], pads.at[0], small, 0)
     small_0(0)
-    small_5(1)
+    reduce_pair(0)
+    small_1(0)
+    reduce_second(1)
+    reduce_first(0)
+    small_4(1)
     halo_finish(3, 3)
-    small_1(0)
+    small_2(0)
     conv_into(pads.at[3], kern_ref, 0, True, emit_mid)
 
     def to_grad_in(it, carry):
@@ -750,17 +780,55 @@
         return carry
 
     lax.fori_loop(0, PIX // 32, to_grad_in, 0)
-    reduce_end(1, mine_1)
-    small_6(1)
-    small_2(0)
     small_3(0)
+    reduce_last(1)
+    small_5(1)
     reduce_second(0)
     small_4(0)
+    mine_1 = reduce_back(1)
+    small_6(1)
     reduce_last(0)
     small_5(0)
+    reduce_end(1, mine_1)
+    small_6(0)
     mine_0 = reduce_back(0)
-    small_6(0)
     reduce_end(0, mine_0)
+
+    for e in range(4):
+        for n, d in enumerate(DIRS):
+
+            @pl.when(exists(d))
+            def _(e=e, n=n):
+                halo_copy(e, n).wait_send()
+
+    for l in range(2):
+        for q in range(4):
+            pair_copy(l, q).wait_send()
+        for k in range(2):
+            relay_copy(l, k).wait_send()
+            first_copy(l, k).wait_send()
+        for k in range(1, 4):
+            second_copy(l, k).wait_send()
+            small_first(l, k).wait_send()
+            small_second(l, k).wait_send()
+            small_gather(l, k).wait_send()
+        for k in range(1, 8):
+            small_z(l, k).wait_send()
+        for q in range(8):
+
+            @pl.when(jnp.logical_not(is_me(last_target(q))))
+            def _(l=l, q=q):
+                last_copy(l, q).wait_send()
+
+        back_copy(l).wait_send()
+        small_pair(l).wait_send()
+        small_back(l).wait_send()
+
+
+def hand_over(*refs):
+    half = len(refs) // 2
+    for src, dst in zip(refs[:half], refs[half:]):
+        dst[...] = src[...]
 
 
 def shards(activations, grad_out, kernels, norm_gains, norm_shifts, w_in, b_in, w_out):
@@ -769,6 +837,8 @@
     dma = pltpu.SemaphoreType.DMA
     pad_size = PROWS * PITCH
     scratch = [
+        pltpu.VMEM((PIX, C), BF16),
+        pltpu.VMEM((7, 7, 2, C), F32),
         pltpu.VMEM((2, C, HID), BF16),
         pltpu.VMEM((2, C, HID), BF16),
         pltpu.VMEM((4, GROUPS, pad_size, 128), F32),
@@ -787,9 +857,11 @@
         pltpu.VMEM((4, 8, 48, C), BF16),
         pltpu.VMEM((2, 4, C, C), BF16),
         pltpu.VMEM((2, 4, C, C), BF16),
-        pltpu.VMEM((2, 3, C, C), BF16),
-        pltpu.VMEM((2, 3, C, C), BF16),
-        pltpu.VMEM((C, C), F32),
+        pltpu.VMEM((2, C, C), BF16),
+        pltpu.VMEM((2, 2, C // 2, C), BF16),
+        pltpu.VMEM((2, 2, C, C), BF16),
+        pltpu.VMEM((2, 2, C, C), BF16),
+        pltpu.VMEM((2, 3, C, C), F32),
         pltpu.VMEM((2, 3, 96, C), BF16),
         pltpu.VMEM((2, 3, 96, C), BF16),
         pltpu.VMEM((96, C), F32),
@@ -805,13 +877,15 @@
         pltpu.VMEM((2, 8, 8, C), F32),
         pltpu.VMEM((2, 4, 8, C), F32),
         pltpu.VMEM((2, 4, 8, C), F32),
-        dma((4,)),
+        dma((7,)),
         dma((4, 8)),
         dma((4, 8)),
         dma((2, 4)),
         dma((2, 4)),
-        dma((2, 3)),
-        dma((2, 3)),
+        dma((2, 2)),
+        dma((2, 2)),
+        dma((2, 2)),
+        dma((2, 2)),
         dma((2, 3)),
         dma((2, 3)),
         dma((2, 8)),
@@ -836,14 +910,14 @@
         kernel,
         out_shape=(
             sds((PIX, C), BF16),
-            sds((2, 7, 7, C), F32),
+            sds((7, 7, 2, C), F32),
             sds((2, C), F32),
             sds((2, C), F32),
             sds((2, HID), F32),
-            sds((2, 8, C), F32),
-            sds((2, 8, C), F32),
+            sds((6, 2, C), F32),
+            sds((6, 2, C), F32),
         ),
-        in_specs=[vmem, vmem, vmem, vmem, vmem, hbm, vmem, hbm],
+        in_specs=[hbm, hbm, hbm, vmem, vmem, hbm, vmem, hbm],
         out_specs=(vmem,) * 7,
         scratch_shapes=scratch,
         compiler_params=pltpu.CompilerParams(
@@ -853,22 +927,28 @@
     )(
         activations.reshape(PIX, C),
         grad_out.reshape(PIX, C),
-        kernels,
+        jnp.transpose(kernels, (1, 2, 0, 3)),
         norm_gains,
         norm_shifts,
         w_in,
         b_in,
         w_out,
     )
-    grad_in, gk, gg, gs, gb, gwi, gwo = outs
+    grad_in, gk, gg, gs, gb, gwi, gwo = pl.pallas_call(
+        hand_over,
+        out_shape=tuple(sds(o.shape, o.dtype) for o in outs),
+        in_specs=[vmem] * 7,
+        out_specs=(vmem,) * 7,
+        name="hand_over",
+    )(*outs)
     return (
         grad_in.reshape(activations.shape),
-        gk,
+        jnp.transpose(gk, (2, 0, 1, 3)),
         gg,
         gs,
         gb,
-        jnp.swapaxes(gwi[:, :6], 1, 2),
-        jnp.swapaxes(gwo[:, :6], 1, 2),
+        jnp.transpose(gwi, (1, 2, 0)),
+        jnp.transpose(gwo, (1, 2, 0)),
     )
 
 

time: 106 us -> 88 us (0.83)
  local copies, waits for them, and re-layouts: 10.7 us -> 0 us
  Pallas kernels: 94.8 us -> 87.2 us
    unnamed x8 -> x0, local copies, waits for them, and re-layouts: 9.93 us -> none
    pallas_call x1 -> x2, Pallas kernels: 94.8 us -> 87.2 us  [the longest x1 85.4 us: shards(): pl.pallas_call(kernel, out_shape=(sds((PIX, C), BF16), sds((7, 7, 2, C),...]
where the time goes in v2:
time: 88 us; the launch traced here: 87.9 us
  Pallas kernels  87.2 us (99%)
    pallas_call x1, Pallas kernels, shards(): pl.pallas_call(kernel, out_shape=(sds((PIX, C), BF16), sds((7, 7, 2, C),...  85.4 us
    pallas_call x1, Pallas kernels, shards(): pl.pallas_call(hand_over, out_shape=tuple((sds(o.shape, o.dtype) for o in...  1.79 us

profile of v2, /device:TPU:1, one launch (start us, length us, event | category | flops | bytes accessed | tf_op | source)
XLA Modules:
  0.0 87.9 jit_solution(10522603131941306209)
XLA Ops:
  0.6 85.4 %convnext_step.1 = (bf16[256,384]{1,0:T(8,128)(2,1)}, f32[7,7,2,384]{3,2,1,0:T(2,128)}, f32[2,384]{1,0:T(2,128)}, f32[2,384]{1,0:T(2,128)}, f32[2,1536]{1,0:T(2,...) custom-call(bf16[256,384]{1,0:T(8,128)(2,1)} %bitcast.7, bf16[256,384]{1,0:T(8,128)(2,1)} %bitcast.8, ...), custom_call_target="tpu_custom_call" | custom-call | tf_op jit(solution)/shard_map/convnext_step/pallas_call | solution.py:909
  86.1 1.8 %hand_over.1 = (bf16[256,384]{1,0:T(8,128)(2,1)}, f32[7,7,2,384]{3,2,1,0:T(2,128)}, f32[2,384]{1,0:T(2,128)}, f32[2,384]{1,0:T(2,128)}, f32[2,1536]{1,0:T(2,128)...) custom-call(bf16[256,384]{1,0:T(8,128)(2,1)} %get-tuple-element.21.refs_0_, f32[7,7,2,384]{3,2,1,0:T(2,128)} %get-tuple-element.22.refs_1_, ...), custom_call_target="tpu_custom_call" | custom-call | tf_op jit(solution)/shard_map/hand_over/pallas_call | solution.py:937

commit v3 on v2

--- a/solution.py
+++ b/solution.py
@@ -97,11 +97,18 @@
     act_hbm,
     gout_hbm,
     kern_hbm,
-    gain_ref,
-    shift_ref,
+    gain_hbm,
+    shift_hbm,
     win_hbm,
-    bin_ref,
+    bin_hbm,
     wout_hbm,
+    gin_hbm,
+    gk_hbm,
+    gg_hbm,
+    gs_hbm,
+    gb_hbm,
+    gwi_hbm,
+    gwo_hbm,
     gin_ref,
     gk_ref,
     gg_ref,
@@ -109,6 +116,9 @@
     gb_ref,
     gwi_ref,
     gwo_ref,
+    gain_ref,
+    shift_ref,
+    bin_ref,
     act_ref,
     kern_ref,
     win,
@@ -124,7 +134,6 @@
     pre_ref,
     dn_ref,
     db_ref,
-    red_ref,
     hsend,
     hrecv,
     csend,
@@ -139,8 +148,6 @@
     own2,
     s3,
     r3,
-    fsend,
-    frecv,
     small,
     smc,
     smt,
@@ -162,8 +169,6 @@
     p2r,
     p3s,
     p3r,
-    fs,
-    fr,
     mcs,
     mcr,
     mas,
@@ -201,10 +206,10 @@
         return device(x, y, (z + k) % 8, core)
 
     def last_target(q):
-        return device(q // 2, first, (q % 2) * 4 + second, core)
-
-    def last_source(zs):
-        return device(zl * (1 - core) + y * core, y * (1 - core) + zl * core, zs, core)
+        return device(q // 4, first, (q // 2 % 2) * 4 + second, q % 2)
+
+    def last_source(q):
+        return device(zl, y, q, 0) if q < 8 else device(y, zl, q - 8, 1)
 
     partner = (r, c + 1 - 2 * core)
 
@@ -223,6 +228,28 @@
     gout_copy = pltpu.make_async_copy(gout_hbm, gn_ref.at[1, 1], wsem.at[6])
     kern_copy.start()
     gout_copy.start()
+    vector_copies = [
+        pltpu.make_async_copy(src, dst, wsem.at[7 + n])
+        for n, (src, dst) in enumerate(
+            ((gain_hbm, gain_ref), (shift_hbm, shift_ref), (bin_hbm, bin_ref))
+        )
+    ]
+    for copy in vector_copies:
+        copy.start()
+    result_copies = [
+        pltpu.make_async_copy(src, dst, wsem.at[10 + n])
+        for n, (src, dst) in enumerate(
+            (
+                (gin_ref, gin_hbm),
+                (gk_ref, gk_hbm),
+                (gg_ref, gg_hbm),
+                (gs_ref, gs_hbm),
+                (gb_ref, gb_hbm),
+                (gwi_ref, gwi_hbm),
+                (gwo_ref, gwo_hbm),
+            )
+        )
+    ]
 
     barrier = pltpu.get_barrier_semaphore()
 
@@ -243,7 +270,7 @@
         greet(second_peer(k))
     for k in range(1, 8):
         greet(z_peer(k))
-    for q in range(8):
+    for q in range(16):
         for dev in (last_target(q), last_source(q)):
             away = jnp.logical_not(is_me(dev))
 
@@ -284,7 +311,7 @@
 
     def halo_copy(e, n):
         d = DIRS[n]
-        size = 32 if d[0] != 0 and d[1] != 0 else 48
+        size = 16 if d[0] != 0 and d[1] != 0 else 48
         return pltpu.make_async_remote_copy(
             src_ref=hsend.at[e, n, pl.ds(0, size)],
             dst_ref=hrecv.at[e, 7 - n, pl.ds(0, size)],
@@ -311,11 +338,12 @@
                         ].astype(BF16)
                 else:
                     col0 = 0 if d[1] < 0 else 8
+                    cut = slice(0, 3) if d[1] < 0 else slice(5, 8)
                     parts = [
                         pads[p, g, pl.ds(pad_row(row0 + k) + col0, 8), :] for k in range(3)
                     ]
-                    hsend[e, n, pl.ds(0, 32), lanes(g)] = jnp.concatenate(
-                        parts + [parts[2]], axis=0
+                    hsend[e, n, pl.ds(0, 16), lanes(g)] = jnp.concatenate(
+                        [v[cut] for v in parts] + [parts[0][0:7]], axis=0
                     ).astype(BF16)
 
             @pl.when(exists(d))
@@ -327,7 +355,7 @@
 
             @pl.when(exists(d))
             def _(n=n, d=d):
-                size = 32 if d[0] != 0 and d[1] != 0 else 48
+                size = 16 if d[0] != 0 and d[1] != 0 else 48
                 pltpu.make_async_remote_copy(
                     src_ref=hsend.at[e, n, pl.ds(0, size)],
                     dst_ref=hrecv.at[e, n, pl.ds(0, size)],
@@ -351,15 +379,17 @@
                                 p, g, pl.ds(pad_row(0) + col0 + k, TILE, stride=PITCH), :
                             ] = got[k * 16 : k * 16 + 16]
                     else:
-                        col0 = -8 if d[1] < 0 else TILE
+                        col0 = -3 if d[1] < 0 else TILE
                         for k in range(3):
-                            pads[p, g, pl.ds(pad_row(row0 + k) + col0, 8), :] = got[
-                                k * 8 : k * 8 + 8
+                            pads[p, g, pl.ds(pad_row(row0 + k) + col0, 3), :] = got[
+                                k * 3 : k * 3 + 3
                             ]
 
     pl.semaphore_wait(barrier, count)
     halo_start(0, 0)
     kern_copy.wait()
+    for copy in vector_copies:
+        copy.wait()
 
     def forward_norm(layer, p):
         def emit(g, i, par, value):
@@ -386,61 +416,65 @@
                 ).astype(BF16)
             return carry
 
-        lax.fori_loop(0, PIX // 32, step, 0)
+        lax.fori_loop(0, PIX // 32, step, 0, unroll=4)
 
     def hidden_forward(layer):
-        def step(n, carry):
-            cols = pl.ds(pl.multiple_of(n * CHUNK, CHUNK), CHUNK)
-            pre_ref[...] = jnp.dot(
-                gn_ref[layer, 0], win[layer, :, cols], preferred_element_type=F32
+        steps = HID // CHUNK
+
+        def product(n):
+            pre_ref[n % 2] = jnp.dot(
+                gn_ref[layer, 0], win[layer, :, n * CHUNK : (n + 1) * CHUNK], preferred_element_type=F32
             )
+
+        product(0)
+        for n in range(steps):
+            cols = pl.ds(n * CHUNK, CHUNK)
+            if n + 1 < steps:
+                product(n + 1)
             bias = bin_ref[pl.ds(layer, 1), cols]
-
-            def inner(it, carry):
-                rows = pl.ds(pl.multiple_of(it * 32, 32), 32)
-                act, slope = gelu_parts(pre_ref[rows, :] + bias)
+            for it in range(PIX // 32):
+                rows = pl.ds(it * 32, 32)
+                act, slope = gelu_parts(pre_ref[n % 2, rows, :] + bias)
                 hid_ref[layer, 1, rows, cols] = act.astype(BF16)
                 slope_ref[layer, rows, cols] = slope
-                return carry
-
-            lax.fori_loop(0, PIX // 32, inner, 0)
-            return carry
-
-        lax.fori_loop(0, HID // CHUNK, step, 0)
 
     def hidden_grad(layer):
-        def step(n, carry):
-            cols = pl.ds(pl.multiple_of(n * CHUNK, CHUNK), CHUNK)
+        for n in range(HID // CHUNK):
+            cols = pl.ds(n * CHUNK, CHUNK)
             ga_ref[:, cols] = jnp.dot(
                 gn_ref[layer, 1], wout[layer, :, cols], preferred_element_type=F32
             )
-            return carry
-
-        lax.fori_loop(0, HID // CHUNK, step, 0)
-
-    def slope_times(layer):
-        def step(n, carry):
-            cols = pl.ds(pl.multiple_of(n * CHUNK, CHUNK), CHUNK)
-
-            def inner(it, total):
-                rows = pl.ds(pl.multiple_of(it * 32, 32), 32)
+
+    def slope_times(layer, matmul):
+        steps = HID // CHUNK
+
+        def product(n):
+            cols = pl.ds(n * CHUNK, CHUNK)
+            ga_ref[:, cols] = jnp.dot(
+                gn_ref[layer, 1], wout[layer, :, cols], preferred_element_type=F32
+            )
+
+        if matmul:
+            product(0)
+        for n in range(steps):
+            cols = pl.ds(n * CHUNK, CHUNK)
+            if matmul and n + 1 < steps:
+                product(n + 1)
+            total = jnp.zeros((8, CHUNK), F32)
+            for it in range(PIX // 32):
+                rows = pl.ds(it * 32, 32)
                 grad = ga_ref[rows, cols] * slope_ref[layer, rows, cols]
                 hid_ref[layer, 0, rows, cols] = grad.astype(BF16)
-                return total + (grad[0:8] + grad[8:16]) + (grad[16:24] + grad[24:32])
-
-            total = lax.fori_loop(0, PIX // 32, inner, jnp.zeros((8, CHUNK), F32))
+                total = total + (grad[0:8] + grad[8:16]) + (grad[16:24] + grad[24:32])
             db_ref[pl.ds(layer, 1), cols] = jnp.sum(total, axis=0, keepdims=True)
-            return carry
-
-        lax.fori_loop(0, HID // CHUNK, step, 0)
 
     def norm_grad(layer, p):
         dn_ref[...] = lax.dot_general(
             hid_ref[layer, 0], win[layer], NT, preferred_element_type=F32
         )
-        red_ref[...] = jnp.zeros_like(red_ref)
 
         def step(it, carry):
+            carry = list(carry)
             rows = pl.ds(pl.multiple_of(it * 32, 32), 32)
             dn = [dn_ref[rows, lanes(g)] for g in range(GROUPS)]
             hat = [hat_ref[layer, g, rows, :] for g in range(GROUPS)]
@@ -457,15 +491,18 @@
                         p, g, pl.ds(pl.multiple_of(pad_row(it * 2 + k), 8), TILE), :
                     ] = dz[k * TILE : (k + 1) * TILE]
                 prod = dn[g] * hat[g]
-                red_ref[0, :, lanes(g)] += (prod[0:8] + prod[8:16]) + (prod[16:24] + prod[24:32])
-                red_ref[1, :, lanes(g)] += (dn[g][0:8] + dn[g][8:16]) + (
-                    dn[g][16:24] + dn[g][24:32]
+                carry[g] += (prod[0:8] + prod[8:16]) + (prod[16:24] + prod[24:32])
+                carry[3 + g] += (dn[g][0:8] + dn[g][8:16]) + (dn[g][16:24] + dn[g][24:32])
+            return tuple(carry)
+
+        sums = lax.fori_loop(
+            0, PIX // 32, step, (jnp.zeros((8, 128), F32),) * 6, unroll=4
+        )
+        for g in range(GROUPS):
+            for k in range(2):
+                small[layer, pl.ds(56 + k, 1), lanes(g)] = jnp.sum(
+                    sums[3 * k + g], axis=0, keepdims=True
                 )
-            return carry
-
-        lax.fori_loop(0, PIX // 32, step, 0)
-        small[layer, pl.ds(56, 1), :] = jnp.sum(red_ref[0], axis=0, keepdims=True)
-        small[layer, pl.ds(57, 1), :] = jnp.sum(red_ref[1], axis=0, keepdims=True)
         for k in range(4):
             small[layer, pl.ds(58 + k, 1), :] = db_ref[pl.ds(layer, 1), pl.ds(k * C, C)]
         small[layer, pl.ds(62, 2), :] = jnp.zeros((2, C), F32)
@@ -497,10 +534,8 @@
         )
 
     def last_copy(l, q):
-        return remote(s3.at[l, q], r3.at[l, z], p3s.at[l, q], p3r.at[l, z], last_target(q))
-
-    def back_copy(l):
-        return remote(fsend.at[l], frecv.at[l], fs.at[l], fr.at[l], partner)
+        slot = core * 8 + z
+        return remote(s3.at[l, q], r3.at[l, slot], p3s.at[l, q], p3r.at[l, slot], last_target(q))
 
     def weight_grad(l, m, q):
         return lax.dot_general(
@@ -511,12 +546,10 @@
         )
 
     def reduce_start(l):
-        def away(q, carry):
+        for k in (2, 3, 1, 0):
+            q = (second + k) % 4
             csend[l, q] = weight_grad(l, 1 - core, q).astype(BF16)
             pair_copy(l, q).start()
-            return carry
-
-        lax.fori_loop(0, 4, away, 0)
 
     def pair_block(l, k):
         q = (first + k) % 4
@@ -530,20 +563,16 @@
             relay_copy(l, k).start()
 
     def reduce_pair(l):
-        def step(i, carry):
-            own1[l, i] = pair_block(l, 1 + 2 * i)
-            return carry
-
-        lax.fori_loop(0, 2, step, 0)
-        own1[l, 2] = pair_block(l, 0)
+        for i, k in enumerate((3, 1, 0)):
+            own1[l, i] = pair_block(l, k)
 
     def reduce_first(l):
         for k in range(2):
             relay_copy(l, k).wait_recv()
             part = pl.ds(192 * k, 192)
             rest = pl.ds(192 * (1 - k), 192)
-            s1[l, k, part, :] = (own1[l, k, part, :] + r0[l, k].astype(F32)).astype(BF16)
-            s1[l, k, rest, :] = own1[l, k, rest, :].astype(BF16)
+            s1[l, k, part, :] = (own1[l, 1 - k, part, :] + r0[l, k].astype(F32)).astype(BF16)
+            s1[l, k, rest, :] = own1[l, 1 - k, rest, :].astype(BF16)
             first_copy(l, k).start()
 
     def reduce_second(l):
@@ -575,9 +604,9 @@
             + r2[l, 1].astype(F32)
             + r2[l, 2].astype(F32)
         )
-        pad = jnp.zeros((4, C), F32)
-        for q in range(8):
-            s3[l, q] = jnp.concatenate([total[12 * q : 12 * q + 12], pad], axis=0).astype(BF16)
+        for q in range(16):
+            piece = total[6 * q : 6 * q + 6]
+            s3[l, q] = jnp.concatenate([piece, piece[0:2]], axis=0).astype(BF16)
             me = is_me(last_target(q))
 
             @pl.when(jnp.logical_not(me))
@@ -586,38 +615,24 @@
 
             @pl.when(me)
             def _(q=q):
-                r3[l, z] = s3[l, q]
-
-    def reduce_back(l):
-        for q in range(8):
+                r3[l, core * 8 + z] = s3[l, q]
+
+    def reduce_end(l):
+        for q in range(16):
 
             @pl.when(jnp.logical_not(is_me(last_source(q))))
             def _(q=q):
                 remote(
-                    s3.at[l, 0], r3.at[l, q], p3s.at[l, 0], p3r.at[l, q], last_source(q)
+                    s3.at[l, q], r3.at[l, q], p3s.at[l, q], p3r.at[l, q], last_source(q)
                 ).wait_recv()
 
-        total = r3[l, 0].astype(F32)
-        for q in range(1, 8):
-            total = total + r3[l, q].astype(F32)
-        total = total * scale
-        pad = jnp.zeros((2, C), F32)
-        low = jnp.concatenate([total[0:6], pad], axis=0)
-        high = jnp.concatenate([total[6:12], pad], axis=0)
-        zeroth = core == 0
-        fsend[l] = jnp.where(zeroth, high, low)
-        back_copy(l).start()
-        return jnp.where(zeroth, low, high)
-
-    def reduce_end(l, mine):
-        back_copy(l).wait_recv()
-        other = frecv[l]
-        zeroth = core == 0
-        wi = jnp.where(zeroth, mine, other)
-        wo = jnp.where(zeroth, other, mine)
-        for j in range(6):
-            gwi_ref[j, pl.ds(l, 1), :] = wi[j : j + 1]
-            gwo_ref[j, pl.ds(l, 1), :] = wo[j : j + 1]
+        for m, out in ((0, gwi_ref), (1, gwo_ref)):
+            total = r3[l, 8 * m].astype(F32)
+            for q in range(1, 8):
+                total = total + r3[l, 8 * m + q].astype(F32)
+            total = total * scale
+            for j in range(6):
+                out[j, pl.ds(l, 1), :] = total[j : j + 1]
 
     def small_pair(l):
         half = pl.ds(pl.multiple_of((1 - core) * 32, 32), 32)
@@ -665,23 +680,25 @@
     def small_2(l):
         for k in range(1, 4):
             small_first(l, k).wait_recv()
-        smb[l, second] = (smt[l, first] + sma[l, 0]) + (sma[l, 1] + sma[l, 2])
+        total = (smt[l, first] + sma[l, 0]) + (sma[l, 1] + sma[l, 2])
+        smb[l, second] = total.astype(BF16)
         for k in range(1, 4):
             small_second(l, k).start()
 
     def small_3(l):
         for k in range(1, 4):
             small_second(l, k).wait_recv()
-        smz[l, z] = (smb[l, 0] + smb[l, 1]) + (smb[l, 2] + smb[l, 3])
+        part = [smb[l, q].astype(F32) for q in range(4)]
+        smz[l, z] = ((part[0] + part[1]) + (part[2] + part[3])).astype(BF16)
         for k in range(1, 8):
             small_z(l, k).start()
 
     def small_4(l):
         for k in range(1, 8):
             small_z(l, k).wait_recv()
-        total = smz[l, 0]
+        total = smz[l, 0].astype(F32)
         for q in range(1, 8):
-            total = total + smz[l, q]
+            total = total + smz[l, q].astype(F32)
         smg[l, first] = total * scale
         for k in range(1, 4):
             small_gather(l, k).start()
@@ -726,14 +743,14 @@
     halo_finish(1, 1)
     forward_norm(1, 1)
     hidden_forward(1)
-    slope_times(1)
+    slope_times(1, False)
     norm_grad(1, 2)
     halo_start(2, 2)
     taps_grad(pads.at[2], pads.at[1], small, 1)
     small_0(1)
     reduce_start(1)
+    reduce_relay(1)
     small_1(1)
-    reduce_relay(1)
     reduce_pair(1)
     halo_finish(2, 2)
 
@@ -751,22 +768,20 @@
         return carry
 
     lax.fori_loop(0, PIX // 32, to_grad_mid, 0)
-    small_2(1)
+    slope_times(0, True)
     reduce_first(1)
-    hidden_grad(0)
-    slope_times(0)
     reduce_start(0)
     norm_grad(0, 3)
     halo_start(3, 3)
-    small_3(1)
     reduce_relay(0)
     taps_grad(pads.at[3], pads.at[0], small, 0)
     small_0(0)
+    small_2(1)
     reduce_pair(0)
     small_1(0)
+    reduce_first(0)
     reduce_second(1)
-    reduce_first(0)
-    small_4(1)
+    small_3(1)
     halo_finish(3, 3)
     small_2(0)
     conv_into(pads.at[3], kern_ref, 0, True, emit_mid)
@@ -780,19 +795,23 @@
         return carry
 
     lax.fori_loop(0, PIX // 32, to_grad_in, 0)
+    result_copies[0].start()
+    reduce_last(1)
+    reduce_second(0)
     small_3(0)
-    reduce_last(1)
+    small_4(1)
+    small_4(0)
     small_5(1)
-    reduce_second(0)
-    small_4(0)
-    mine_1 = reduce_back(1)
-    small_6(1)
     reduce_last(0)
     small_5(0)
-    reduce_end(1, mine_1)
+    small_6(1)
+    reduce_end(1)
     small_6(0)
-    mine_0 = reduce_back(0)
-    reduce_end(0, mine_0)
+    for copy in result_copies[1:5]:
+        copy.start()
+    reduce_end(0)
+    for copy in result_copies[5:]:
+        copy.start()
 
     for e in range(4):
         for n, d in enumerate(DIRS):
@@ -814,29 +833,46 @@
             small_gather(l, k).wait_send()
         for k in range(1, 8):
             small_z(l, k).wait_send()
-        for q in range(8):
+        for q in range(16):
 
             @pl.when(jnp.logical_not(is_me(last_target(q))))
             def _(l=l, q=q):
                 last_copy(l, q).wait_send()
 
-        back_copy(l).wait_send()
         small_pair(l).wait_send()
         small_back(l).wait_send()
+    for copy in result_copies:
+        copy.wait()
 
 
 def hand_over(*refs):
-    half = len(refs) // 2
-    for src, dst in zip(refs[:half], refs[half:]):
-        dst[...] = src[...]
+    srcs, dsts, mids, sem = refs[:7], refs[7:14], refs[14:21], refs[21]
+    ins = [pltpu.make_async_copy(u, v, sem.at[n]) for n, (u, v) in enumerate(zip(srcs, mids))]
+    outs = [pltpu.make_async_copy(u, v, sem.at[7 + n]) for n, (u, v) in enumerate(zip(mids, dsts))]
+    for copy in ins:
+        copy.start()
+    for copy, then in zip(ins, outs):
+        copy.wait()
+        then.start()
+    for copy in outs:
+        copy.wait()
 
 
 def shards(activations, grad_out, kernels, norm_gains, norm_shifts, w_in, b_in, w_out):
-    vmem = pl.BlockSpec(memory_space=pltpu.VMEM)
     hbm = pl.BlockSpec(memory_space=pl.ANY)
     dma = pltpu.SemaphoreType.DMA
     pad_size = PROWS * PITCH
     scratch = [
+        pltpu.VMEM((PIX, C), BF16),
+        pltpu.VMEM((7, 7, 2, C), F32),
+        pltpu.VMEM((2, C), F32),
+        pltpu.VMEM((2, C), F32),
+        pltpu.VMEM((2, HID), F32),
+        pltpu.VMEM((6, 2, C), F32),
+        pltpu.VMEM((6, 2, C), F32),
+        pltpu.VMEM((2, C), F32),
+        pltpu.VMEM((2, C), F32),
+        pltpu.VMEM((2, HID), F32),
         pltpu.VMEM((PIX, C), BF16),
         pltpu.VMEM((7, 7, 2, C), F32),
         pltpu.VMEM((2, C, HID), BF16),
@@ -849,10 +885,9 @@
         pltpu.VMEM((2, 2, PIX, C), BF16),
         pltpu.VMEM((2, PIX, HID), F32),
         pltpu.VMEM((PIX, HID), F32),
-        pltpu.VMEM((PIX, CHUNK), F32),
+        pltpu.VMEM((2, PIX, CHUNK), F32),
         pltpu.VMEM((PIX, C), F32),
         pltpu.VMEM((2, HID), F32),
-        pltpu.VMEM((2, 8, C), F32),
         pltpu.VMEM((4, 8, 48, C), BF16),
         pltpu.VMEM((4, 8, 48, C), BF16),
         pltpu.VMEM((2, 4, C, C), BF16),
@@ -865,19 +900,17 @@
         pltpu.VMEM((2, 3, 96, C), BF16),
         pltpu.VMEM((2, 3, 96, C), BF16),
         pltpu.VMEM((96, C), F32),
-        pltpu.VMEM((2, 8, 16, C), BF16),
-        pltpu.VMEM((2, 8, 16, C), BF16),
-        pltpu.VMEM((2, 8, C), F32),
-        pltpu.VMEM((2, 8, C), F32),
+        pltpu.VMEM((2, 16, 8, C), BF16),
+        pltpu.VMEM((2, 16, 8, C), BF16),
         pltpu.VMEM((2, SMALL, C), F32),
         pltpu.VMEM((2, 32, C), F32),
         pltpu.VMEM((2, 4, 8, C), F32),
         pltpu.VMEM((2, 3, 8, C), F32),
-        pltpu.VMEM((2, 4, 8, C), F32),
-        pltpu.VMEM((2, 8, 8, C), F32),
+        pltpu.VMEM((2, 4, 8, C), BF16),
+        pltpu.VMEM((2, 8, 8, C), BF16),
         pltpu.VMEM((2, 4, 8, C), F32),
         pltpu.VMEM((2, 4, 8, C), F32),
-        dma((7,)),
+        dma((17,)),
         dma((4, 8)),
         dma((4, 8)),
         dma((2, 4)),
@@ -888,10 +921,8 @@
         dma((2, 2)),
         dma((2, 3)),
         dma((2, 3)),
-        dma((2, 8)),
-        dma((2, 8)),
-        dma((2,)),
-        dma((2,)),
+        dma((2, 16)),
+        dma((2, 16)),
         dma((2,)),
         dma((2,)),
         dma((2, 3)),
@@ -917,8 +948,8 @@
             sds((6, 2, C), F32),
             sds((6, 2, C), F32),
         ),
-        in_specs=[hbm, hbm, hbm, vmem, vmem, hbm, vmem, hbm],
-        out_specs=(vmem,) * 7,
+        in_specs=[hbm] * 8,
+        out_specs=(hbm,) * 7,
         scratch_shapes=scratch,
         compiler_params=pltpu.CompilerParams(
             collective_id=0, has_side_effects=True, vmem_limit_bytes=64000000
@@ -937,8 +968,9 @@
     grad_in, gk, gg, gs, gb, gwi, gwo = pl.pallas_call(
         hand_over,
         out_shape=tuple(sds(o.shape, o.dtype) for o in outs),
-        in_specs=[vmem] * 7,
-        out_specs=(vmem,) * 7,
+        in_specs=[hbm] * 7,
+        out_specs=(hbm,) * 7,
+        scratch_shapes=[pltpu.VMEM(o.shape, o.dtype) for o in outs] + [dma((14,))],
         name="hand_over",
     )(*outs)
     return (

time: 88 us -> 74.4 us (0.85)
  Pallas kernels: 87.2 us -> 73.6 us
    pallas_call x1, Pallas kernels: 85.4 us -> 71.8 us  [shards(): pl.pallas_call(kernel, out_shape=(sds((PIX, C), BF16), sds((7, 7, 2, C),...]
where the time goes in v3:
time: 74.4 us; the launch traced here: 74.3 us
  Pallas kernels  73.6 us (99%)
    pallas_call x1, Pallas kernels, shards(): pl.pallas_call(kernel, out_shape=(sds((PIX, C), BF16), sds((7, 7, 2, C),...  71.8 us
    pallas_call x1, Pallas kernels, shards(): pl.pallas_call(hand_over, out_shape=tuple((sds(o.shape, o.dtype) for o in...  1.81 us

profile of v3, /device:TPU:1, one launch (start us, length us, event | category | flops | bytes accessed | tf_op | source)
XLA Modules:
  0.0 74.3 jit_solution(1723922680595976223)
XLA Ops:
  0.6 71.8 %convnext_step.1 = (bf16[256,384]{1,0:T(8,128)(2,1)}, f32[7,7,2,384]{3,2,1,0:T(2,128)}, f32[2,384]{1,0:T(2,128)}, f32[2,384]{1,0:T(2,128)}, f32[2,1536]{1,0:T(2,...) custom-call(bf16[256,384]{1,0:T(8,128)(2,1)} %bitcast.7, bf16[256,384]{1,0:T(8,128)(2,1)} %bitcast.8, ...), custom_call_target="tpu_custom_call" | custom-call | tf_op jit(solution)/shard_map/convnext_step/pallas_call | solution.py:940
  72.5 1.8 %hand_over.1 = (bf16[256,384]{1,0:T(8,128)(2,1)}, f32[7,7,2,384]{3,2,1,0:T(2,128)}, f32[2,384]{1,0:T(2,128)}, f32[2,384]{1,0:T(2,128)}, f32[2,1536]{1,0:T(2,128)...) custom-call(bf16[256,384]{1,0:T(8,128)(2,1)} %get-tuple-element.21.refs_0_, f32[7,7,2,384]{3,2,1,0:T(2,128)} %get-tuple-element.22.refs_1_, ...), custom_call_target="tpu_custom_call" | custom-call | tf_op jit(solution)/shard_map/hand_over/pallas_call | solution.py:968

commit v4 on v3

--- a/solution.py
+++ b/solution.py
@@ -71,6 +71,57 @@
         return carry
 
     lax.fori_loop(0, GROUPS * (TILE // block), step, 0)
+
+
+def conv_sides(src, kern, layer, out):
+    def step(g, carry):
+        col = pl.ds(pl.multiple_of(g * 128, 128), 128)
+        for side in range(2):
+            acc = {}
+            for q in range(3):
+                at = 5 + q if side == 0 else 24 + q
+                for a in range(7):
+                    for half in range(2):
+                        v = src[g, pl.ds((a + 8 * half) * PITCH + at, 8, stride=PITCH), :]
+                        for j in range(3):
+                            b = q - j if side == 0 else 6 + q - j
+                            if b < 0 or b > 6:
+                                continue
+                            term = v * kern[a, b, pl.ds(layer, 1), col]
+                            key = (j, half)
+                            acc[key] = term if key not in acc else acc[key] + term
+            for (j, half), value in acc.items():
+                own = j if side == 0 else 13 + j
+                at = pl.ds(8 * half * TILE + own, 8, stride=TILE)
+                out[g, at, :] = out[g, at, :] + value
+        return carry
+
+    lax.fori_loop(0, GROUPS, step, 0)
+
+
+def conv_ends(src, kern, layer, out):
+    def step(g, carry):
+        col = pl.ds(pl.multiple_of(g * 128, 128), 128)
+        for rhos in (range(0, 3), range(19, 22)):
+            acc = {}
+            for rho in rhos:
+                taps = [src[g, pl.ds(rho * PITCH + 5 + s, 8, stride=2), :] for s in range(8)]
+                for a in range(7):
+                    i = rho - a
+                    if i < 0 or i >= TILE:
+                        continue
+                    for b in range(7):
+                        w = kern[a, b, pl.ds(layer, 1), col]
+                        for par in range(2):
+                            term = taps[b + par] * w
+                            key = (i, par)
+                            acc[key] = term if key not in acc else acc[key] + term
+            for (i, par), value in acc.items():
+                at = pl.ds(i * TILE + par, 8, stride=2)
+                out[g, at, :] = out[g, at, :] + value
+        return carry
+
+    lax.fori_loop(0, GROUPS, step, 0)
 
 
 def taps_grad(grad, src, small, layer):
@@ -315,8 +366,8 @@
         return pltpu.make_async_remote_copy(
             src_ref=hsend.at[e, n, pl.ds(0, size)],
             dst_ref=hrecv.at[e, 7 - n, pl.ds(0, size)],
-            send_sem=hs.at[e, n],
-            recv_sem=hr.at[e, 7 - n],
+            send_sem=hs.at[n],
+            recv_sem=hr.at[e % 2, 7 - n],
             device_id=(r + d[0], c + d[1]),
             device_id_type=MESH,
         )
@@ -350,8 +401,10 @@
             def _(n=n):
                 halo_copy(e, n).start()
 
-    def halo_finish(e, p):
+    def halo_finish(e, p, sides=(True, False)):
         for n, d in enumerate(DIRS):
+            if (d[0] == 0) not in sides:
+                continue
 
             @pl.when(exists(d))
             def _(n=n, d=d):
@@ -359,8 +412,8 @@
                 pltpu.make_async_remote_copy(
                     src_ref=hsend.at[e, n, pl.ds(0, size)],
                     dst_ref=hrecv.at[e, n, pl.ds(0, size)],
-                    send_sem=hs.at[e, n],
-                    recv_sem=hr.at[e, n],
+                    send_sem=hs.at[n],
+                    recv_sem=hr.at[e % 2, n],
                     device_id=(r + d[0], c + d[1]),
                     device_id_type=MESH,
                 ).wait_recv()
@@ -391,12 +444,19 @@
     for copy in vector_copies:
         copy.wait()
 
-    def forward_norm(layer, p):
+    def forward_conv(layer, p):
         def emit(g, i, par, value):
             z_ref[g, pl.ds(i * TILE + par, 8, stride=2), :] = value
 
         conv_into(pads.at[p], kern_ref, layer, False, emit)
 
+    def halo_conv(layer, e, p):
+        halo_finish(e, p, (True,))
+        conv_sides(pads.at[p], kern_ref, layer, z_ref)
+        halo_finish(e, p, (False,))
+        conv_ends(pads.at[p], kern_ref, layer, z_ref)
+
+    def forward_norm(layer, p):
         def step(it, carry):
             rows = pl.ds(pl.multiple_of(it * 32, 32), 32)
             zs = [z_ref[g, rows, :] for g in range(GROUPS)]
@@ -518,24 +578,36 @@
         )
 
     def pair_copy(l, q):
-        return remote(csend.at[l, q], crecv.at[l, q], cs.at[l, q], cr.at[l, q], partner)
+        return remote(csend.at[l, q], crecv.at[l, q], cs.at[l], cr.at[l, q], partner)
 
     def relay_copy(l, k):
         return remote(
-            s0.at[l, pl.ds(192 * k, 192)], r0.at[l, k], p0s.at[l, k], p0r.at[l, k], first_peer(1 + 2 * k)
+            s0.at[l, pl.ds(192 * k, 192)], r0.at[l, k], p0s.at[l], p0r.at[l, k], first_peer(1 + 2 * k)
         )
 
     def first_copy(l, k):
-        return remote(s1.at[l, k], r1.at[l, k], p1s.at[l, k], p1r.at[l, k], first_peer(1 + 2 * k))
+        return remote(s1.at[l, k], r1.at[l, k], p1s.at[l], p1r.at[l], first_peer(1 + 2 * k))
 
     def second_copy(l, k):
         return remote(
-            s2.at[l, k - 1], r2.at[l, k - 1], p2s.at[l, k - 1], p2r.at[l, k - 1], second_peer(k)
+            s2.at[l, k - 1], r2.at[l, k - 1], p2s.at[l], p2r.at[l], second_peer(k)
         )
 
     def last_copy(l, q):
         slot = core * 8 + z
-        return remote(s3.at[l, q], r3.at[l, slot], p3s.at[l, q], p3r.at[l, slot], last_target(q))
+        return remote(s3.at[l, q], r3.at[l, slot], p3s.at[l], p3r.at[l], last_target(q))
+
+    def first_all(l):
+        return remote(s1.at[l], r1.at[l], p1s.at[l], p1r.at[l], partner)
+
+    def second_all(l):
+        return remote(s2.at[l], r2.at[l], p2s.at[l], p2r.at[l], partner)
+
+    def last_all(l, n):
+        part = pl.ds(0, n)
+        return remote(s3.at[l, part], r3.at[l, part], p3s.at[l], p3r.at[l], partner)
+
+    keeps = jnp.logical_and(first == y, second == zl)
 
     def weight_grad(l, m, q):
         return lax.dot_general(
@@ -576,8 +648,7 @@
             first_copy(l, k).start()
 
     def reduce_second(l):
-        for k in range(2):
-            first_copy(l, k).wait_recv()
+        first_all(l).wait_recv()
 
         def block(k):
             rows = pl.ds(pl.multiple_of(((second + k) % 4) * 96, 96), 96)
@@ -596,8 +667,7 @@
         own2[...] = block(0)
 
     def reduce_last(l):
-        for k in range(1, 4):
-            second_copy(l, k).wait_recv()
+        second_all(l).wait_recv()
         total = (
             own2[...]
             + r2[l, 0].astype(F32)
@@ -618,13 +688,13 @@
                 r3[l, core * 8 + z] = s3[l, q]
 
     def reduce_end(l):
-        for q in range(16):
-
-            @pl.when(jnp.logical_not(is_me(last_source(q))))
-            def _(q=q):
-                remote(
-                    s3.at[l, q], r3.at[l, q], p3s.at[l, q], p3r.at[l, q], last_source(q)
-                ).wait_recv()
+        @pl.when(jnp.logical_not(keeps))
+        def _():
+            last_all(l, 16).wait_recv()
+
+        @pl.when(keeps)
+        def _():
+            last_all(l, 15).wait_recv()
 
         for m, out in ((0, gwi_ref), (1, gwo_ref)):
             total = r3[l, 8 * m].astype(F32)
@@ -641,30 +711,45 @@
     def small_first(l, k):
         q = (first + k) % 4
         return remote(
-            smt.at[l, q], sma.at[l, k - 1], mas.at[l, k - 1], mar.at[l, k - 1], first_peer(k)
+            smt.at[l, q], sma.at[l, k - 1], mas.at[l], mar.at[l], first_peer(k)
         )
 
     def small_second(l, k):
         return remote(
             smb.at[l, second],
             smb.at[l, second],
-            mbs.at[l, k - 1],
-            mbr.at[l, k - 1],
+            mbs.at[l],
+            mbr.at[l],
             second_peer(k),
         )
 
     def small_z(l, k):
         return remote(
-            smz.at[l, z], smz.at[l, z], mzs.at[l, k - 1], mzr.at[l, k - 1], z_peer(k)
+            smz.at[l, z], smz.at[l, z], mzs.at[l], mzr.at[l], z_peer(k)
         )
 
     def small_gather(l, k):
         return remote(
-            smg.at[l, first], smg.at[l, first], mgs.at[l, k - 1], mgr.at[l, k - 1], first_peer(k)
+            smg.at[l, first], smg.at[l, first], mgs.at[l], mgr.at[l], first_peer(k)
         )
 
     def small_back(l):
         return remote(smg.at[l], smx.at[l], mxs.at[l], mxr.at[l], partner)
+
+    def small_first_all(l):
+        return remote(smt.at[l, pl.ds(0, 3)], sma.at[l], mas.at[l], mar.at[l], partner)
+
+    def small_second_all(l):
+        part = smb.at[l, pl.ds(0, 3)]
+        return remote(part, part, mbs.at[l], mbr.at[l], partner)
+
+    def small_z_all(l):
+        part = smz.at[l, pl.ds(0, 7)]
+        return remote(part, part, mzs.at[l], mzr.at[l], partner)
+
+    def small_gather_all(l):
+        part = smg.at[l, pl.ds(0, 3)]
+        return remote(part, part, mgs.at[l], mgr.at[l], partner)
 
     def small_0(l):
         small_pair(l).start()
@@ -678,24 +763,21 @@
             small_first(l, k).start()
 
     def small_2(l):
-        for k in range(1, 4):
-            small_first(l, k).wait_recv()
+        small_first_all(l).wait_recv()
         total = (smt[l, first] + sma[l, 0]) + (sma[l, 1] + sma[l, 2])
         smb[l, second] = total.astype(BF16)
         for k in range(1, 4):
             small_second(l, k).start()
 
     def small_3(l):
-        for k in range(1, 4):
-            small_second(l, k).wait_recv()
+        small_second_all(l).wait_recv()
         part = [smb[l, q].astype(F32) for q in range(4)]
         smz[l, z] = ((part[0] + part[1]) + (part[2] + part[3])).astype(BF16)
         for k in range(1, 8):
             small_z(l, k).start()
 
     def small_4(l):
-        for k in range(1, 8):
-            small_z(l, k).wait_recv()
+        small_z_all(l).wait_recv()
         total = smz[l, 0].astype(F32)
         for q in range(1, 8):
             total = total + smz[l, q].astype(F32)
@@ -704,8 +786,7 @@
             small_gather(l, k).start()
 
     def small_5(l):
-        for k in range(1, 4):
-            small_gather(l, k).wait_recv()
+        small_gather_all(l).wait_recv()
         small_back(l).start()
 
     def small_6(l):
@@ -722,7 +803,8 @@
         for k in range(4):
             gb_ref[pl.ds(l, 1), pl.ds(k * C, C)] = full[58 + k : 59 + k]
 
-    halo_finish(0, 0)
+    forward_conv(0, 0)
+    halo_conv(0, 0, 0)
     forward_norm(0, 0)
     for copy in weight_copies:
         copy.wait()
@@ -740,7 +822,8 @@
     halo_start(1, 1)
     gout_copy.wait()
     hidden_grad(1)
-    halo_finish(1, 1)
+    forward_conv(1, 1)
+    halo_conv(1, 1, 1)
     forward_norm(1, 1)
     hidden_forward(1)
     slope_times(1, False)
@@ -813,31 +896,31 @@
     for copy in result_copies[5:]:
         copy.start()
 
-    for e in range(4):
-        for n, d in enumerate(DIRS):
-
-            @pl.when(exists(d))
-            def _(e=e, n=n):
-                halo_copy(e, n).wait_send()
+    for n, d in enumerate(DIRS):
+
+        @pl.when(exists(d))
+        def _(n=n, d=d):
+            size = 16 if d[0] != 0 and d[1] != 0 else 48
+            part = hsend.at[pl.ds(0, 4), n, pl.ds(0, size)]
+            remote(part, part, hs.at[n], hr.at[0, n], partner).wait_send()
 
     for l in range(2):
-        for q in range(4):
-            pair_copy(l, q).wait_send()
-        for k in range(2):
-            relay_copy(l, k).wait_send()
-            first_copy(l, k).wait_send()
-        for k in range(1, 4):
-            second_copy(l, k).wait_send()
-            small_first(l, k).wait_send()
-            small_second(l, k).wait_send()
-            small_gather(l, k).wait_send()
-        for k in range(1, 8):
-            small_z(l, k).wait_send()
-        for q in range(16):
-
-            @pl.when(jnp.logical_not(is_me(last_target(q))))
-            def _(l=l, q=q):
-                last_copy(l, q).wait_send()
+        remote(csend.at[l], crecv.at[l], cs.at[l], cr.at[l, 0], partner).wait_send()
+        remote(s0.at[l], s0.at[l], p0s.at[l], p0r.at[l, 0], partner).wait_send()
+        first_all(l).wait_send()
+        second_all(l).wait_send()
+        small_first_all(l).wait_send()
+        small_second_all(l).wait_send()
+        small_z_all(l).wait_send()
+        small_gather_all(l).wait_send()
+
+        @pl.when(jnp.logical_not(keeps))
+        def _(l=l):
+            last_all(l, 16).wait_send()
+
+        @pl.when(keeps)
+        def _(l=l):
+            last_all(l, 15).wait_send()
 
         small_pair(l).wait_send()
         small_back(l).wait_send()
@@ -911,31 +994,13 @@
         pltpu.VMEM((2, 4, 8, C), F32),
         pltpu.VMEM((2, 4, 8, C), F32),
         dma((17,)),
-        dma((4, 8)),
-        dma((4, 8)),
+        dma((8,)),
+        dma((2, 8)),
+        dma((2,)),
         dma((2, 4)),
-        dma((2, 4)),
+        dma((2,)),
         dma((2, 2)),
-        dma((2, 2)),
-        dma((2, 2)),
-        dma((2, 2)),
-        dma((2, 3)),
-        dma((2, 3)),
-        dma((2, 16)),
-        dma((2, 16)),
-        dma((2,)),
-        dma((2,)),
-        dma((2, 3)),
-        dma((2, 3)),
-        dma((2, 3)),
-        dma((2, 3)),
-        dma((2, 7)),
-        dma((2, 7)),
-        dma((2, 3)),
-        dma((2, 3)),
-        dma((2,)),
-        dma((2,)),
-    ]
+    ] + [dma((2,))] * 18
     sds = jax.ShapeDtypeStruct
     outs = pl.pallas_call(
         kernel,

time: 74.4 us -> 70.8 us (0.952)
  Pallas kernels: 73.6 us -> 70 us
    pallas_call x1, Pallas kernels: 71.8 us -> 68.2 us  [shards(): pl.pallas_call(kernel, out_shape=(sds((PIX, C), BF16), sds((7, 7, 2, C),...]
where the time goes in v4:
time: 70.8 us; the launch traced here: 70.7 us
  Pallas kernels  70 us (99%)
    pallas_call x1, Pallas kernels, shards(): pl.pallas_call(kernel, out_shape=(sds((PIX, C), BF16), sds((7, 7, 2, C),...  68.2 us
    pallas_call x1, Pallas kernels, shards(): pl.pallas_call(hand_over, out_shape=tuple((sds(o.shape, o.dtype) for o in...  1.81 us

profile of v4, /device:TPU:1, one launch (start us, length us, event | category | flops | bytes accessed | tf_op | source)
XLA Modules:
  0.0 70.7 jit_solution(9947301867496365116)
XLA Ops:
  0.6 68.2 %convnext_step.1 = (bf16[256,384]{1,0:T(8,128)(2,1)}, f32[7,7,2,384]{3,2,1,0:T(2,128)}, f32[2,384]{1,0:T(2,128)}, f32[2,384]{1,0:T(2,128)}, f32[2,1536]{1,0:T(2,...) custom-call(bf16[256,384]{1,0:T(8,128)(2,1)} %bitcast.7, bf16[256,384]{1,0:T(8,128)(2,1)} %bitcast.8, ...), custom_call_target="tpu_custom_call" | custom-call | tf_op jit(solution)/shard_map/convnext_step/pallas_call | solution.py:1005
  68.8 1.8 %hand_over.1 = (bf16[256,384]{1,0:T(8,128)(2,1)}, f32[7,7,2,384]{3,2,1,0:T(2,128)}, f32[2,384]{1,0:T(2,128)}, f32[2,384]{1,0:T(2,128)}, f32[2,1536]{1,0:T(2,128)...) custom-call(bf16[256,384]{1,0:T(8,128)(2,1)} %get-tuple-element.21.refs_0_, f32[7,7,2,384]{3,2,1,0:T(2,128)} %get-tuple-element.22.refs_1_, ...), custom_call_target="tpu_custom_call" | custom-call | tf_op jit(solution)/shard_map/hand_over/pallas_call | solution.py:1033

commit v5 on v4

--- a/solution.py
+++ b/solution.py
@@ -851,8 +851,8 @@
         return carry
 
     lax.fori_loop(0, PIX // 32, to_grad_mid, 0)
+    reduce_first(1)
     slope_times(0, True)
-    reduce_first(1)
     reduce_start(0)
     norm_grad(0, 3)
     halo_start(3, 3)

time: 70.8 us -> 70.2 us (level)
  no operation moved by 1% of the time
where the time goes in v5:
time: 70.2 us; the launch traced here: 70.1 us
  Pallas kernels  69.4 us (99%)
    pallas_call x1, Pallas kernels, shards(): pl.pallas_call(kernel, out_shape=(sds((PIX, C), BF16), sds((7, 7, 2, C),...  67.6 us
    pallas_call x1, Pallas kernels, shards(): pl.pallas_call(hand_over, out_shape=tuple((sds(o.shape, o.dtype) for o in...  1.81 us

profile of v5, /device:TPU:1, one launch (start us, length us, event | category | flops | bytes accessed | tf_op | source)
XLA Modules:
  0.0 70.1 jit_solution(8517919472061390385)
XLA Ops:
  0.6 67.6 %convnext_step.1 = (bf16[256,384]{1,0:T(8,128)(2,1)}, f32[7,7,2,384]{3,2,1,0:T(2,128)}, f32[2,384]{1,0:T(2,128)}, f32[2,384]{1,0:T(2,128)}, f32[2,1536]{1,0:T(2,...) custom-call(bf16[256,384]{1,0:T(8,128)(2,1)} %bitcast.7, bf16[256,384]{1,0:T(8,128)(2,1)} %bitcast.8, ...), custom_call_target="tpu_custom_call" | custom-call | tf_op jit(solution)/shard_map/convnext_step/pallas_call | solution.py:1005
  68.3 1.8 %hand_over.1 = (bf16[256,384]{1,0:T(8,128)(2,1)}, f32[7,7,2,384]{3,2,1,0:T(2,128)}, f32[2,384]{1,0:T(2,128)}, f32[2,384]{1,0:T(2,128)}, f32[2,1536]{1,0:T(2,128)...) custom-call(bf16[256,384]{1,0:T(8,128)(2,1)} %get-tuple-element.21.refs_0_, f32[7,7,2,384]{3,2,1,0:T(2,128)} %get-tuple-element.22.refs_1_, ...), custom_call_target="tpu_custom_call" | custom-call | tf_op jit(solution)/shard_map/hand_over/pallas_call | solution.py:1033
